TPU v7x, 512 devices: a whole 4x8x8 slice. The times are simulated.
512 devices in a mesh: dp: 16 (over x_hi, y), mp: 32 (over z, x_lo, core).
Axes of the slice: x: 4 (x_hi: 2, x_lo: 2; x = x_hi * 2 + x_lo), y: 8, z: 8, core: 2. Of those that a mesh axis runs over, the one named last changes fastest.
Arguments:
- frames: bfloat16 [4096, 1536], P('dp', 'mp'), may hold values from -6 to 6
- conv_kernel: bfloat16 [32, 1536], P(None, 'mp'), may hold values from -1 to 1
- head_weight: bfloat16 [1536, 16384], P(None, 'mp'), may hold values from -13 to 13
- utterance_ids: int32 [16, 256], P('dp'), may hold values from 0 to 3, never falling along the last dimension, each value on 1 to 128 neighbouring positions
- tile_used: int32 [16], P('dp'), may hold values from 128 to 256
- teacher_ids: int32 [4096, 32], P('dp'), may hold values from 0 to 16383, all different within a row
- teacher_logits: int32 [4096, 32], P('dp'), may hold values from -127 to 127
- teacher_scale: float32 [4096], P('dp'), may hold values from 0.03 to 3
Outputs:
- input_grad: float32 [4096, 1536], P('dp', 'mp')
- kernel_grad: float32 [32, 1536], P(None, 'mp')
- head_grad: float32 [1536, 16384], P('dp', 'mp')
All inputs are finite; a program needn't handle non-finite values.
Results may differ from a plain program's by a relative error of at most 0.02.
The roundings to bfloat16 on the way count: a program that leaves them out, or rounds other values in their place, can miss the bound.
Values may be sent and summed in bfloat16 or wider, within the bound.
A program may use at most 64 MiB of HBM per device.

v0:
```python
import jax
import jax.numpy as jnp
from jax import lax
from jax.sharding import Mesh
from jax.sharding import PartitionSpec as P

KERNEL = 32
DP = ("dp_0", "dp_1")


def joined_along(blocks, dim):
    shape = list(blocks.shape[1:])
    shape[dim] *= blocks.shape[0]
    return jnp.moveaxis(blocks, 0, dim).reshape(shape)


def sent_to_all(value, axis):
    devices = lax.axis_size(axis)
    return lax.all_to_all(
        jnp.broadcast_to(value[None], (devices, *value.shape)), axis, 0, 0, tiled=True
    )


def collect(value, axis, dim):
    return joined_along(sent_to_all(value, axis), dim)


def all_in_one(value, axis):
    leaves = jax.tree.leaves(value)
    turns = sorted(range(len(leaves)), key=lambda k: -leaves[k].size)
    width = (1, *leaves[turns[0]].shape)[-1]
    lines = [
        jnp.pad(leaves[k].reshape(-1), (0, -leaves[k].size % width)).reshape(-1, width)
        for k in turns
    ]
    both, at, found = (sent_to_all(jnp.concatenate(lines), axis), 0, {})
    for k, line in zip(turns, lines):
        section = both[:, at : at + len(line)].reshape(len(both), -1)
        found[k] = section[:, : leaves[k].size].reshape(-1, *leaves[k].shape)
        at += len(line)
    numbers = iter(range(len(leaves)))
    return jax.tree.map(lambda _: found[next(numbers)], value)


def folded_in_pairs(pieces, combine):
    while len(jax.tree.leaves(pieces)[0]) > 1:
        pieces = jax.vmap(combine)(
            *(jax.tree.map(lambda part: part[side::2], pieces) for side in (0, 1))
        )
    return jax.tree.map(lambda part: part[0], pieces)


def combined_all(value, axis, combine):
    pieces = all_in_one(value, axis)
    return folded_in_pairs(pieces, combine)


def sum_in_order(blocks, axes, turns):
    shape = [lax.axis_size(a) for a in axes]
    blocks = blocks.reshape(*shape, *blocks.shape[1:])
    blocks = blocks.transpose(*turns, *range(len(axes), blocks.ndim))
    blocks = blocks.reshape(-1, *blocks.shape[len(axes) :])
    for k in turns:
        blocks = lax.psum_scatter(blocks, axes[k], scatter_dimension=0, tiled=True)
    return blocks[0]


def cut_along(value, dim, devices):
    shape = value.shape
    blocks = value.reshape(*shape[:dim], devices, shape[dim] // devices, *shape[dim + 1 :])
    return jnp.moveaxis(blocks, dim, 0)


def scatter_axes(value, axes, turns, dim):
    devices = lax.axis_size(axes)
    return sum_in_order(cut_along(value, dim, devices), axes, turns)


def summed_on_arrival(value, axis, dim):
    devices = lax.axis_size(axis)
    blocks = lax.all_to_all(cut_along(value, dim, devices), axis, 0, 0, tiled=True)
    return jnp.sum(blocks.astype(jnp.float32), axis=0)


def over_copies(value, axis):
    return sent_to_all(value, axis).sum(axis=0)


def conv_tile(source, taps, seg_row, valid_row):
    count = source.shape[0]
    left = (KERNEL - 1) // 2
    right = KERNEL - 1 - left
    padded = jnp.pad(source, ((left, right), (0, 0)))
    seg_pad = jnp.pad(seg_row, (left, right), constant_values=-1)
    valid_pad = jnp.pad(valid_row, (left, right), constant_values=False)
    result = jnp.zeros(source.shape, jnp.float32)
    for tap in range(KERNEL):
        keep = (seg_pad[tap : tap + count] == seg_row) & valid_pad[tap : tap + count] & valid_row
        result = result + jnp.where(keep[:, None], padded[tap : tap + count] * taps[tap], 0.0)
    return result


def softmax_pair(first, second):
    peak = jnp.maximum(first[0], second[0])
    return (peak, first[1] * jnp.exp(first[0] - peak) + second[1] * jnp.exp(second[0] - peak))


def local(
    frames,
    conv_kernel,
    head_weight,
    utterance_ids,
    tile_used,
    teacher_ids,
    teacher_logits,
    teacher_scale,
):
    seg_row = utterance_ids[0]
    used = tile_used[0]
    count = frames.shape[0]
    block = head_weight.shape[1]
    valid = jnp.arange(count, dtype=jnp.int32) < used
    kern = conv_kernel.astype(jnp.float32)

    def convolve(values, taps):
        return conv_tile(values, taps, seg_row, valid)

    conv_own = convolve(frames.astype(jnp.float32), kern).astype(jnp.bfloat16)
    conv = collect(conv_own, "mp", 1)
    logits = jnp.dot(conv, head_weight, preferred_element_type=jnp.float32)
    local_peak = jnp.max(logits, axis=1)
    local_total = jnp.sum(jnp.exp(logits - local_peak[:, None]), axis=1)
    peak, total = combined_all((local_peak, local_total), "mp", softmax_pair)
    normaliser = peak + jnp.log(total)
    teacher = jax.nn.softmax(teacher_scale[:, None] * teacher_logits.astype(jnp.float32), axis=1)
    first_piece = lax.axis_index("mp") * block
    local_ids = teacher_ids - first_piece
    inside = (local_ids >= 0) & (local_ids < block)
    rowpos = jnp.arange(count, dtype=jnp.int32)[:, None]
    target = (
        jnp.zeros((count, block), jnp.float32)
        .at[rowpos, jnp.clip(local_ids, 0, block - 1)]
        .add(jnp.where(inside, teacher, 0.0))
    )
    logit_grad = jnp.where(
        valid[:, None], jnp.exp(logits - normaliser[:, None]) - target, 0.0
    ).astype(jnp.bfloat16)
    head_grad = scatter_axes(
        lax.dot_general(
            conv, logit_grad, (((0,), (0,)), ((), ())), preferred_element_type=jnp.float32
        ).astype(jnp.bfloat16),
        DP,
        (1, 0),
        0,
    ).astype(jnp.float32)
    conv_grad_t = summed_on_arrival(
        lax.dot_general(
            head_weight, logit_grad, (((1,), (1,)), ((), ())), preferred_element_type=jnp.float32
        ).astype(jnp.bfloat16),
        "mp",
        0,
    )
    conv_grad = conv_grad_t.T
    _, pull = jax.vjp(convolve, frames.astype(jnp.float32), kern)
    input_grad, kernel_part = pull(conv_grad)
    kernel_grad = over_copies(kernel_part, DP)
    return (input_grad, kernel_grad, head_grad)


def solution(mesh):
    finer = Mesh(mesh.devices.reshape(2, 8, mesh.shape["mp"]), ("dp_0", "dp_1", "mp"))
    return jax.shard_map(
        local,
        mesh=finer,
        in_specs=(
            P(DP, "mp"),
            P(None, "mp"),
            P(None, "mp"),
            P(DP, None),
            P(DP),
            P(DP, None),
            P(DP, None),
            P(DP),
        ),
        out_specs=(P(DP, "mp"), P(None, "mp"), P(DP, "mp")),
        check_vma=False,
    )
```

profile of v0, /device:TPU:1, one launch (start us, length us, event | category | flops | bytes accessed | tf_op | source)
XLA Modules:
  0.0 198.4 jit_solution(3940165625930709168)
XLA Ops:
  7.2 0.0 copy-start
  7.2 0.0 copy-start.84
  7.2 0.0 copy-start.83
  7.2 0.8 convert_element_type.39
  8.0 0.6 slice_bitcast_fusion.31
  8.7 0.6 slice_bitcast_fusion.30
  9.4 0.7 convert_element_type.38
  10.8 1.0 and_and_fusion.24
  11.8 0.8 and_and_fusion
  12.7 1.0 and_and_fusion.29
  13.7 1.0 and_and_fusion.28
  14.7 1.0 and_and_fusion.27
  15.7 1.0 and_and_fusion.26
  16.8 1.0 and_and_fusion.25
  17.8 0.0 copy-start.1
  17.8 0.0 copy-start.4
  17.8 1.6 add_convert_fusion
  19.4 0.9 broadcast_in_dim.577
  20.4 12.9 %all-to-all-start = ((bf16[32,256,48]{1,2,0:T(8,128)(2,1)}), bf16[32,256,48]{1,2,0:T(8,128)(2,1)S(1)}, u32[]{:S(2)}, u32[]{:S(2)}) async-start(bf16[32,256,48]{1,2,0:T(8,128)(2,1)} %broadcast_in_dim.577), calls=%async_computation | async-start | bytes 1572864 | tf_op jit(solution)/shard_map/all_to_all | solution.py:19
  33.5 0.1 multiply_reduce_fusion
  33.6 0.1 and_reduce_fusion
  33.7 0.1 copy.24
  34.0 0.7 reshape.292
  34.7 21.1 %all-to-all-done = bf16[32,256,48]{1,2,0:T(8,128)(2,1)S(1)} async-done(((bf16[32,256,48]{1,2,0:T(8,128)(2,1)}), bf16[32,256,48]{1,2,0:T(8,128)(2,1)S(1)}, u32[]{:S(2)}, u32[]{:S(2)}) %all-to-all-start) | async-done | bytes 786464 | tf_op jit(solution)/shard_map/all_to_all | solution.py:19
  55.8 0.7 fusion.42
  56.5 0.2 exponential_reduce_fusion
  56.7 0.7 broadcast_in_dim.578
  57.4 4.7 %all-to-all-start.1 = ((f32[32,2,256]{2,1,0:T(2,128)}), f32[32,2,256]{2,1,0:T(2,128)S(1)}, u32[]{:S(2)}, u32[]{:S(2)}) async-start(f32[32,2,256]{2,1,0:T(2,128)} %broadcast_in_dim.578), calls=%async_computation.1 | async-start | bytes 131072 | tf_op jit(solution)/shard_map/all_to_all | solution.py:19
  62.0 0.0 reduce-scatter.3.cloned.1.call-start
  62.1 0.1 copy.25
  62.2 0.7 reshape.294
  62.9 56.8 %scatter_custom_fusion = f32[131072]{0:T(1024)S(1)} fusion(s32[8192]{0:T(1024)} %reshape.292, f32[8192]{0:T(1024)} %reshape.294, f32[]{:T(128)} %constant.56.clone.1), kind=kCustom, calls=%fused_computation.38 | custom fusion | flops 8192 | bytes 524800
  119.8 0.9 reshape.290
  120.6 0.1 fusion.41
  121.1 1.2 select_convert_fusion
  122.3 0.6 convolution_convert_fusion
  122.9 1.3 copy.27
  124.2 0.0 reduce-scatter.3.cloned.1.call-update
  124.2 0.0 reduce-scatter.5.cloned.1.call-start
  124.2 0.6 fusion
  124.9 0.3 copy.26
  125.5 30.7 %all_to_all.20 = bf16[32,48,256]{2,1,0:T(8,128)(2,1)S(1)} all-to-all(bf16[32,48,256]{2,1,0:T(8,128)(2,1)S(1)} %bitcast.300), channel_id=1, replica_groups=mesh['dp_0'=2,'dp_1'=8,'mp'=32] {'mp'}, dimensions={0} | all-to-all | bytes 1572864 | tf_op jit(solution)/shard_map/all_to_all | solution.py:81
  156.3 0.1 convert_reduce_fusion
  156.5 0.4 fusion.15
  157.0 0.4 fusion.25
  157.4 0.4 fusion.34
  158.0 0.3 fusion.6
  158.4 0.1 bitcast_multiply_fusion.59
  158.5 0.8 bitcast_multiply_fusion.63
  159.3 0.8 bitcast_multiply_fusion.61
  160.2 4.0 %reduce-scatter.3.cloned.1.call-done = bf16[2,96,512]{2,1,0:T(8,128)(2,1)} async-done(((bf16[16,96,512]{2,1,0:T(8,128)(2,1)}), bf16[2,96,512]{2,1,0:T(8,128)(2,1)}) %reduce-scatter.3.cloned.1.call-update) | async-done | bytes 196624 | tf_op jit(solution)/shard_map/reduce_scatter | solution.py:64
  164.2 0.0 reduce-scatter.5.cloned.1.call-update
  164.2 0.1 pad_add_fusion.8
  164.3 0.9 reshape.300
  165.2 7.2 %all-to-all-start.3 = ((f32[16,1,1536]{2,1,0:T(1,128)}), f32[16,1,1536]{2,1,0:T(1,128)S(1)}, u32[]{:S(2)}, u32[]{:S(2)}) async-start(f32[16,1,1536]{2,1,0:T(1,128)} %reshape.300), calls=%async_computation.3 | async-start | bytes 196608 | tf_op jit(solution)/shard_map/all_to_all | solution.py:19
  172.4 0.6 pad_add_fusion
  173.0 0.8 pad_add_fusion.2
  173.7 7.6 %all-to-all-done.3 = f32[16,1,1536]{2,1,0:T(1,128)S(1)} async-done(((f32[16,1,1536]{2,1,0:T(1,128)}), f32[16,1,1536]{2,1,0:T(1,128)S(1)}, u32[]{:S(2)}, u32[]{:S(2)}) %all-to-all-start.3) | async-done | bytes 98336 | tf_op jit(solution)/shard_map/all_to_all | solution.py:19
  181.3 0.5 broadcast.268
  181.8 0.9 reduce.4
  182.7 0.1 reshape.301
  182.8 0.6 reduce_sum.377
  183.5 6.5 %reduce-scatter.5.cloned.1.call-done = bf16[1,96,512]{2,1,0:T(8,128)(2,1)} async-done(((bf16[2,96,512]{2,1,0:T(8,128)(2,1)}), bf16[1,96,512]{2,1,0:T(8,128)(2,1)}) %reduce-scatter.5.cloned.1.call-update) | async-done | bytes 98320 | tf_op jit(solution)/shard_map/reduce_scatter | solution.py:64
  190.0 1.6 bitcast_convert_fusion
  (198 shorter events, 0.9 us)
Async XLA Ops:
  7.2 48.6 %copy-start = (bf16[1536,512]{1,0:T(8,128)(2,1)S(1)}, bf16[1536,512]{1,0:T(8,128)(2,1)}, u32[]{:S(2)}) copy-start(bf16[1536,512]{1,0:T(8,128)(2,1)} %param.10) | copy-start | bytes 4718596
  7.2 26.3 %copy-start.84 = (s32[2]{0:T(128)S(1)}, s32[2]{0:T(128)}, u32[]{:S(2)}) copy-start(s32[2]{0:T(128)} %constant.200) | copy-start | bytes 28
  7.2 26.4 %copy-start.83 = (s32[2]{0:T(128)S(1)}, s32[2]{0:T(128)}, u32[]{:S(2)}) copy-start(s32[2]{0:T(128)} %constant.203) | copy-start | bytes 28
  7.2 26.2 %copy-start.2 = (s32[256,32]{0,1:T(8,128)S(1)}, s32[256,32]{0,1:T(8,128)}, u32[]{:S(2)}) copy-start(s32[256,32]{0,1:T(8,128)} %param.13) | copy-start | bytes 98308
  8.7 25.1 %copy-start.45 = (f32[48]{0:T(128)}, f32[48]{0:T(128)S(1)}, u32[]{:S(2)}) copy-start(f32[48]{0:T(128)S(1)} %get-tuple-element.80) | copy-start | bytes 580
  8.7 25.1 %copy-start.47 = (f32[48]{0:T(128)}, f32[48]{0:T(128)S(1)}, u32[]{:S(2)}) copy-start(f32[48]{0:T(128)S(1)} %get-tuple-element.81) | copy-start | bytes 580
  8.7 25.1 %copy-start.49 = (f32[48]{0:T(128)}, f32[48]{0:T(128)S(1)}, u32[]{:S(2)}) copy-start(f32[48]{0:T(128)S(1)} %get-tuple-element.82) | copy-start | bytes 580
  8.7 25.2 %copy-start.51 = (f32[48]{0:T(128)}, f32[48]{0:T(128)S(1)}, u32[]{:S(2)}) copy-start(f32[48]{0:T(128)S(1)} %get-tuple-element.83) | copy-start | bytes 580
  8.7 25.2 %copy-start.53 = (f32[48]{0:T(128)}, f32[48]{0:T(128)S(1)}, u32[]{:S(2)}) copy-start(f32[48]{0:T(128)S(1)} %get-tuple-element.84) | copy-start | bytes 580
  8.7 25.2 %copy-start.55 = (f32[48]{0:T(128)}, f32[48]{0:T(128)S(1)}, u32[]{:S(2)}) copy-start(f32[48]{0:T(128)S(1)} %get-tuple-element.85) | copy-start | bytes 580
  8.7 25.2 %copy-start.57 = (f32[48]{0:T(128)}, f32[48]{0:T(128)S(1)}, u32[]{:S(2)}) copy-start(f32[48]{0:T(128)S(1)} %get-tuple-element.86) | copy-start | bytes 580
  8.7 25.2 %copy-start.59 = (f32[48]{0:T(128)}, f32[48]{0:T(128)S(1)}, u32[]{:S(2)}) copy-start(f32[48]{0:T(128)S(1)} %get-tuple-element.87) | copy-start | bytes 580
  8.7 25.2 %copy-start.61 = (f32[48]{0:T(128)}, f32[48]{0:T(128)S(1)}, u32[]{:S(2)}) copy-start(f32[48]{0:T(128)S(1)} %get-tuple-element.77) | copy-start | bytes 580
  8.7 25.2 %copy-start.63 = (f32[48]{0:T(128)}, f32[48]{0:T(128)S(1)}, u32[]{:S(2)}) copy-start(f32[48]{0:T(128)S(1)} %get-tuple-element.94) | copy-start | bytes 580
  9.4 24.5 %copy-start.75 = (f32[48]{0:T(128)}, f32[48]{0:T(128)S(1)}, u32[]{:S(2)}) copy-start(f32[48]{0:T(128)S(1)} %get-tuple-element.96) | copy-start | bytes 580
  9.4 24.5 %copy-start.77 = (f32[48]{0:T(128)}, f32[48]{0:T(128)S(1)}, u32[]{:S(2)}) copy-start(f32[48]{0:T(128)S(1)} %get-tuple-element.106) | copy-start | bytes 580
  9.4 24.5 %copy-start.79 = (f32[48]{0:T(128)}, f32[48]{0:T(128)S(1)}, u32[]{:S(2)}) copy-start(f32[48]{0:T(128)S(1)} %get-tuple-element.107) | copy-start | bytes 580
  9.4 24.5 %copy-start.81 = (f32[48]{0:T(128)}, f32[48]{0:T(128)S(1)}, u32[]{:S(2)}) copy-start(f32[48]{0:T(128)S(1)} %get-tuple-element.108) | copy-start | bytes 580
  11.8 21.5 %copy-start.25 = (pred[256]{0:T(512)(128)(4,1)}, pred[256]{0:T(512)(128)(4,1)S(1)}, u32[]{:S(2)}) copy-start(pred[256]{0:T(512)(128)(4,1)S(1)} %get-tuple-element.134) | copy-start | bytes 772
  20.4 35.4 %all-to-all-start = ((bf16[32,256,48]{1,2,0:T(8,128)(2,1)}), bf16[32,256,48]{1,2,0:T(8,128)(2,1)S(1)}, u32[]{:S(2)}, u32[]{:S(2)}) async-start(bf16[32,256,48]{1,2,0:T(8,128)(2,1)} %broadcast_in_dim.577), calls=%async_computation | async-start | bytes 1572864 | tf_op jit(solution)/shard_map/all_to_all | solution.py:19
  57.4 63.3 %all-to-all-start.1 = ((f32[32,2,256]{2,1,0:T(2,128)}), f32[32,2,256]{2,1,0:T(2,128)S(1)}, u32[]{:S(2)}, u32[]{:S(2)}) async-start(f32[32,2,256]{2,1,0:T(2,128)} %broadcast_in_dim.578), calls=%async_computation.1 | async-start | bytes 131072 | tf_op jit(solution)/shard_map/all_to_all | solution.py:19
  62.0 102.2 %reduce-scatter.3.cloned.1.call-start = ((), (), s32[]{:S(2)}) async-start(), calls=%async_computation.6 | async-start | bytes 1769472 | tf_op jit(solution)/shard_map/reduce_scatter | solution.py:64
  124.2 65.8 %reduce-scatter.5.cloned.1.call-start = ((), (), s32[]{:S(2)}) async-start(), calls=%async_computation.7 | async-start | bytes 294912 | tf_op jit(solution)/shard_map/reduce_scatter | solution.py:64
  125.1 31.2 %copy-start.8 = (pred[256]{0:T(512)(128)(4,1)S(1)}, pred[256]{0:T(512)(128)(4,1)}, u32[]{:S(2)}) copy-start(pred[256]{0:T(512)(128)(4,1)} %copy-done.7) | copy-start | bytes 772
  125.1 31.2 %copy-start.26 = (pred[256]{0:T(512)(128)(4,1)S(1)}, pred[256]{0:T(512)(128)(4,1)}, u32[]{:S(2)}) copy-start(pred[256]{0:T(512)(128)(4,1)} %copy-done.25) | copy-start | bytes 772
  125.2 31.2 %copy-start.28 = (pred[256]{0:T(512)(128)(4,1)S(1)}, pred[256]{0:T(512)(128)(4,1)}, u32[]{:S(2)}) copy-start(pred[256]{0:T(512)(128)(4,1)} %copy-done.27) | copy-start | bytes 772
  125.2 31.2 %copy-start.30 = (pred[256]{0:T(512)(128)(4,1)S(1)}, pred[256]{0:T(512)(128)(4,1)}, u32[]{:S(2)}) copy-start(pred[256]{0:T(512)(128)(4,1)} %copy-done.29) | copy-start | bytes 772
  125.2 31.2 %copy-start.32 = (pred[256]{0:T(512)(128)(4,1)S(1)}, pred[256]{0:T(512)(128)(4,1)}, u32[]{:S(2)}) copy-start(pred[256]{0:T(512)(128)(4,1)} %copy-done.31) | copy-start | bytes 772
  125.2 31.2 %copy-start.36 = (pred[256]{0:T(512)(128)(4,1)S(1)}, pred[256]{0:T(512)(128)(4,1)}, u32[]{:S(2)}) copy-start(pred[256]{0:T(512)(128)(4,1)} %copy-done.35) | copy-start | bytes 772
  125.2 31.2 %copy-start.38 = (pred[256]{0:T(512)(128)(4,1)S(1)}, pred[256]{0:T(512)(128)(4,1)}, u32[]{:S(2)}) copy-start(pred[256]{0:T(512)(128)(4,1)} %copy-done.37) | copy-start | bytes 772
  125.2 31.2 %copy-start.40 = (pred[256]{0:T(512)(128)(4,1)S(1)}, pred[256]{0:T(512)(128)(4,1)}, u32[]{:S(2)}) copy-start(pred[256]{0:T(512)(128)(4,1)} %copy-done.39) | copy-start | bytes 772
  125.2 31.2 %copy-start.42 = (pred[256]{0:T(512)(128)(4,1)S(1)}, pred[256]{0:T(512)(128)(4,1)}, u32[]{:S(2)}) copy-start(pred[256]{0:T(512)(128)(4,1)} %copy-done.41) | copy-start | bytes 772
  125.2 31.7 %copy-start.6 = (pred[256]{0:T(512)(128)(4,1)S(1)}, pred[256]{0:T(512)(128)(4,1)}, u32[]{:S(2)}) copy-start(pred[256]{0:T(512)(128)(4,1)} %copy-done.5) | copy-start | bytes 772
  125.2 31.7 %copy-start.10 = (pred[256]{0:T(512)(128)(4,1)S(1)}, pred[256]{0:T(512)(128)(4,1)}, u32[]{:S(2)}) copy-start(pred[256]{0:T(512)(128)(4,1)} %copy-done.9) | copy-start | bytes 772
  125.2 31.7 %copy-start.12 = (pred[256]{0:T(512)(128)(4,1)S(1)}, pred[256]{0:T(512)(128)(4,1)}, u32[]{:S(2)}) copy-start(pred[256]{0:T(512)(128)(4,1)} %copy-done.11) | copy-start | bytes 772
  125.3 31.7 %copy-start.14 = (pred[256]{0:T(512)(128)(4,1)S(1)}, pred[256]{0:T(512)(128)(4,1)}, u32[]{:S(2)}) copy-start(pred[256]{0:T(512)(128)(4,1)} %copy-done.13) | copy-start | bytes 772
  125.3 31.7 %copy-start.16 = (pred[256]{0:T(512)(128)(4,1)S(1)}, pred[256]{0:T(512)(128)(4,1)}, u32[]{:S(2)}) copy-start(pred[256]{0:T(512)(128)(4,1)} %copy-done.15) | copy-start | bytes 772
  125.3 31.7 %copy-start.18 = (pred[256]{0:T(512)(128)(4,1)S(1)}, pred[256]{0:T(512)(128)(4,1)}, u32[]{:S(2)}) copy-start(pred[256]{0:T(512)(128)(4,1)} %copy-done.17) | copy-start | bytes 772
  125.3 31.7 %copy-start.20 = (pred[256]{0:T(512)(128)(4,1)S(1)}, pred[256]{0:T(512)(128)(4,1)}, u32[]{:S(2)}) copy-start(pred[256]{0:T(512)(128)(4,1)} %copy-done.19) | copy-start | bytes 772
  125.3 31.7 %copy-start.22 = (pred[256]{0:T(512)(128)(4,1)S(1)}, pred[256]{0:T(512)(128)(4,1)}, u32[]{:S(2)}) copy-start(pred[256]{0:T(512)(128)(4,1)} %copy-done.21) | copy-start | bytes 772
  125.3 31.7 %copy-start.24 = (pred[256]{0:T(512)(128)(4,1)S(1)}, pred[256]{0:T(512)(128)(4,1)}, u32[]{:S(2)}) copy-start(pred[256]{0:T(512)(128)(4,1)} %copy-done.23) | copy-start | bytes 772
  125.3 32.1 %copy-start.34 = (pred[256]{0:T(512)(128)(4,1)S(1)}, pred[256]{0:T(512)(128)(4,1)}, u32[]{:S(2)}) copy-start(pred[256]{0:T(512)(128)(4,1)} %copy-done.33) | copy-start | bytes 772
  125.3 32.1 %copy-start.44 = (pred[256]{0:T(512)(128)(4,1)S(1)}, pred[256]{0:T(512)(128)(4,1)}, u32[]{:S(2)}) copy-start(pred[256]{0:T(512)(128)(4,1)} %copy-done.43) | copy-start | bytes 772
  125.3 32.5 %copy-start.3 = (bf16[256,48]{0,1:T(8,128)(2,1)S(1)}, bf16[256,48]{0,1:T(8,128)(2,1)}, u32[]{:S(2)}) copy-start(bf16[256,48]{0,1:T(8,128)(2,1)} %param.8) | copy-start | bytes 73732
  125.3 32.5 %copy-start.62 = (f32[48]{0:T(128)S(1)}, f32[48]{0:T(128)}, u32[]{:S(2)}) copy-start(f32[48]{0:T(128)} %copy-done.61) | copy-start | bytes 580
  125.4 32.5 %copy-start.64 = (f32[48]{0:T(128)S(1)}, f32[48]{0:T(128)}, u32[]{:S(2)}) copy-start(f32[48]{0:T(128)} %copy-done.63) | copy-start | bytes 580
  125.4 32.5 %copy-start.66 = (pred[256]{0:T(512)(128)(4,1)S(1)}, pred[256]{0:T(512)(128)(4,1)}, u32[]{:S(2)}) copy-start(pred[256]{0:T(512)(128)(4,1)} %copy-done.65) | copy-start | bytes 772
  125.4 32.5 %copy-start.68 = (pred[256]{0:T(512)(128)(4,1)S(1)}, pred[256]{0:T(512)(128)(4,1)}, u32[]{:S(2)}) copy-start(pred[256]{0:T(512)(128)(4,1)} %copy-done.67) | copy-start | bytes 772
  125.4 32.5 %copy-start.70 = (pred[256]{0:T(512)(128)(4,1)S(1)}, pred[256]{0:T(512)(128)(4,1)}, u32[]{:S(2)}) copy-start(pred[256]{0:T(512)(128)(4,1)} %copy-done.69) | copy-start | bytes 772
  125.4 32.5 %copy-start.72 = (pred[256]{0:T(512)(128)(4,1)S(1)}, pred[256]{0:T(512)(128)(4,1)}, u32[]{:S(2)}) copy-start(pred[256]{0:T(512)(128)(4,1)} %copy-done.71) | copy-start | bytes 772
  125.4 32.5 %copy-start.74 = (pred[256]{0:T(512)(128)(4,1)S(1)}, pred[256]{0:T(512)(128)(4,1)}, u32[]{:S(2)}) copy-start(pred[256]{0:T(512)(128)(4,1)} %copy-done.73) | copy-start | bytes 772
  125.4 32.5 %copy-start.76 = (f32[48]{0:T(128)S(1)}, f32[48]{0:T(128)}, u32[]{:S(2)}) copy-start(f32[48]{0:T(128)} %copy-done.75) | copy-start | bytes 580
  125.4 32.5 %copy-start.78 = (f32[48]{0:T(128)S(1)}, f32[48]{0:T(128)}, u32[]{:S(2)}) copy-start(f32[48]{0:T(128)} %copy-done.77) | copy-start | bytes 580
  125.4 32.5 %copy-start.80 = (f32[48]{0:T(128)S(1)}, f32[48]{0:T(128)}, u32[]{:S(2)}) copy-start(f32[48]{0:T(128)} %copy-done.79) | copy-start | bytes 580
  125.4 32.5 %copy-start.82 = (f32[48]{0:T(128)S(1)}, f32[48]{0:T(128)}, u32[]{:S(2)}) copy-start(f32[48]{0:T(128)} %copy-done.81) | copy-start | bytes 580
  125.5 32.8 %copy-start.46 = (f32[48]{0:T(128)S(1)}, f32[48]{0:T(128)}, u32[]{:S(2)}) copy-start(f32[48]{0:T(128)} %copy-done.45) | copy-start | bytes 580
  125.5 32.8 %copy-start.48 = (f32[48]{0:T(128)S(1)}, f32[48]{0:T(128)}, u32[]{:S(2)}) copy-start(f32[48]{0:T(128)} %copy-done.47) | copy-start | bytes 580
  125.5 32.8 %copy-start.50 = (f32[48]{0:T(128)S(1)}, f32[48]{0:T(128)}, u32[]{:S(2)}) copy-start(f32[48]{0:T(128)} %copy-done.49) | copy-start | bytes 580
  125.5 32.8 %copy-start.52 = (f32[48]{0:T(128)S(1)}, f32[48]{0:T(128)}, u32[]{:S(2)}) copy-start(f32[48]{0:T(128)} %copy-done.51) | copy-start | bytes 580
  125.5 32.8 %copy-start.54 = (f32[48]{0:T(128)S(1)}, f32[48]{0:T(128)}, u32[]{:S(2)}) copy-start(f32[48]{0:T(128)} %copy-done.53) | copy-start | bytes 580
  125.5 32.8 %copy-start.56 = (f32[48]{0:T(128)S(1)}, f32[48]{0:T(128)}, u32[]{:S(2)}) copy-start(f32[48]{0:T(128)} %copy-done.55) | copy-start | bytes 580
  125.5 32.8 %copy-start.58 = (f32[48]{0:T(128)S(1)}, f32[48]{0:T(128)}, u32[]{:S(2)}) copy-start(f32[48]{0:T(128)} %copy-done.57) | copy-start | bytes 580
  125.5 32.8 %copy-start.60 = (f32[48]{0:T(128)S(1)}, f32[48]{0:T(128)}, u32[]{:S(2)}) copy-start(f32[48]{0:T(128)} %copy-done.59) | copy-start | bytes 580
  165.2 16.1 %all-to-all-start.3 = ((f32[16,1,1536]{2,1,0:T(1,128)}), f32[16,1,1536]{2,1,0:T(1,128)S(1)}, u32[]{:S(2)}, u32[]{:S(2)}) async-start(f32[16,1,1536]{2,1,0:T(1,128)} %reshape.300), calls=%async_computation.3 | async-start | bytes 196608 | tf_op jit(solution)/shard_map/all_to_all | solution.py:19
  (26 other events, 472.6 us)
Sparse Core Ops, SparseCore 0:
  124.3 39.8 reduce-scatter.2
  167.0 22.9 reduce-scatter.4
where the time goes:
time: 199 us; the launch traced here: 198 us
  other arithmetic  76.6 us (38%)
  waiting for transfers between devices  39.2 us (20%)
  blocking collectives  30.7 us (15%)
  starting transfers between devices  24.8 us (12%)
  between operations  16.2 us (8%)
  local copies, waits for them, and re-layouts  9.11 us (5%)
    unnamed x4, other arithmetic  57 us
    all_to_all x1, blocking collectives, summed_on_arrival(): lax.all_to_all(cut_along(value, dim, devices), axis, 0, 0, tiled=True)  30.7 us
    all_to_all x3, waiting for transfers between devices, sent_to_all(): lax.all_to_all(jnp.broadcast_to(value[None], (devices, *value.shape)), ax...  28.6 us
    all_to_all x3, starting transfers between devices, sent_to_all(): lax.all_to_all(jnp.broadcast_to(value[None], (devices, *value.shape)), ax...  24.7 us
    reduce_scatter x2, waiting for transfers between devices, sum_in_order(): blocks = lax.psum_scatter(blocks, axes[k], scatter_dimension=0, tiled=True)  10.6 us
    and x7, other arithmetic, conv_tile(): (seg_pad[tap:tap + count] == seg_row) & valid_pad[tap:tap + count]  6.75 us
  transfers between devices with their start and end apart: 5, of which 4 were waited for; matrix products, arithmetic and copies ran while one was open for 34% of the time, Pallas kernels for 0%

commit v1 on v0

v1 whole, which is shorter than its diff:
```python
import functools

import jax
import jax.numpy as jnp
from jax import lax
from jax.experimental import pallas as pl
from jax.experimental.pallas import tpu as pltpu
from jax.sharding import PartitionSpec as P

MESH = pl.DeviceIdType.MESH
TAPS = 32
LEFT = (TAPS - 1) // 2
TOP = 32
NZ = 8
NY = 8
CH = 48
T = 256
VOC = 512
ZX = 16
F32 = jnp.float32
BF = jnp.bfloat16

NEAR = (1, 7, 2, 6, 3, 5, 4)
FAR = (4, 3, 5, 2, 6, 1, 7)


def eye(n):
    same = lax.broadcasted_iota(jnp.int32, (n, n), 0) == lax.broadcasted_iota(jnp.int32, (n, n), 1)
    return jnp.where(same, 1.0, 0.0).astype(BF)


def turned(values):
    return lax.dot_general(
        eye(values.shape[1]), values, (((1,), (1,)), ((), ())), preferred_element_type=F32
    )


def kernel(
    frames, taps, w_hbm, seg, used, ids, tlog, scale,
    out_in, out_k, out_h,
    w, wt, conv, xt, src_rows, dst_rows, rel_ids, teach, tgt, ex, stats, gt,
    cg, cin, xsend, xin, zsend, zin,
    hh, rin, xfin, xrin, kg, kx, ky,
    w_sem, a_send, a_recv, b_send, b_recv, dc_send, dc_recv, dx_send, dx_recv, dz_send, dz_recv,
    r_send, r_recv, cx_send, cx_recv, k_send, k_recv,
):
    m = lax.axis_index("mp")
    d = lax.axis_index("dp")
    c, xl, z = m % 2, (m // 2) % 2, m // 4
    y, xh = d % NY, d // NY
    zx = m // 2
    oc, ox, oh = 1 - c, 1 - xl, 1 - xh
    core_peer = {"mp": m + 1 - 2 * c}
    x_peer = {"mp": m + 2 - 4 * xl}
    h_peer = {"dp": oh * NY + y}

    def z_at(off):
        return (z + off) % NZ

    def z_peer(off):
        return {"mp": z_at(off) * 4 + xl * 2 + c}

    def y_at(off):
        return (y + off + NY) % NY

    def y_peer(off):
        return {"dp": xh * NY + y_at(off)}

    load_w = pltpu.make_async_copy(w_hbm, w, w_sem)
    load_w.start()

    barrier = pltpu.get_barrier_semaphore()

    @pl.loop(1, 32)
    def _(off):
        pl.semaphore_signal(barrier, inc=1, device_id={"mp": (m + off) % 32}, device_id_type=MESH)

    for off in range(1, NY):
        pl.semaphore_signal(barrier, inc=1, device_id=y_peer(off), device_id_type=MESH)
    pl.semaphore_signal(barrier, inc=1, device_id=h_peer, device_id_type=MESH)

    def remote(src, dst, send, recv, peer):
        return pltpu.make_async_remote_copy(
            src_ref=src, dst_ref=dst, send_sem=send, recv_sem=recv, device_id=peer, device_id_type=MESH
        )

    lane = lax.broadcasted_iota(jnp.int32, (8, T), 1)
    valid = lane < used[0]
    seg_rows = jnp.broadcast_to(seg[...], (8, T))
    src_rows[...] = jnp.where(valid, seg_rows, -1)
    dst_rows[...] = jnp.where(valid, seg_rows, -2)
    xt[...] = turned(frames[...])
    tap_t = turned(taps[...])

    def kept(delta):
        rolled = src_rows[...]
        if delta:
            rolled = pltpu.roll(rolled, (-delta) % T, 1)
        keep = rolled == dst_rows[...]
        if delta > 0:
            keep = keep & (lane < T - delta)
        if delta < 0:
            keep = keep & (lane >= -delta)
        return keep

    def moved(values, delta):
        return pltpu.roll(values, (-delta) % T, 1) if delta else values

    def only(keep, values):
        return jnp.where(keep[None], values.reshape(CH // 8, 8, T), 0.0).reshape(CH, T)

    acc = jnp.zeros((CH, T), F32)
    for j in range(TAPS):
        delta = j - LEFT
        acc = acc + only(kept(delta), moved(xt[...], delta) * tap_t[:, j : j + 1])
    conv[c, zx] = acc.astype(BF)

    pl.semaphore_wait(barrier, 31 + NY)

    def a_copy(slot_c, slot_zx, k, peer):
        return remote(
            conv.at[slot_c, slot_zx], conv.at[slot_c, slot_zx], a_send.at[k], a_recv.at[slot_c, slot_zx], peer
        )

    sent = []
    for k, off in enumerate(FAR):
        copy = a_copy(c, zx, k, z_peer(off))
        copy.start()
        sent.append(copy)
    copy = a_copy(c, zx, 7, x_peer)
    copy.start()
    sent.append(copy)
    copy = a_copy(c, zx, 8, core_peer)
    copy.start()
    sent.append(copy)

    load_w.wait()
    for half in range(2):
        for v in range(VOC // 128):
            part = w[:, half, :, v * 128 : (v + 1) * 128].reshape(ZX * CH, 128)
            wt[half, v * 128 : (v + 1) * 128, :] = part.T

    def teacher_work():
        upper = turned((ids[...] // 128).astype(F32).astype(BF))
        lower = turned((ids[...] % 128).astype(F32).astype(BF))
        rel_ids[...] = upper.astype(jnp.int32) * 128 + lower.astype(jnp.int32) - m * VOC
        scores = scale[...].reshape(1, T) * turned(tlog[...].astype(F32).astype(BF))
        top = jnp.exp(scores - jnp.max(scores, axis=0, keepdims=True))
        teach[...] = top / jnp.sum(top, axis=0, keepdims=True)

        @pl.loop(0, VOC // 64)
        def _(part):
            first = pl.multiple_of(part * 64, 64)
            row = lax.broadcasted_iota(jnp.int32, (64, T), 0) + first
            found = jnp.zeros((64, T), F32)
            for k in range(TOP):
                found = jnp.where(row == rel_ids[k : k + 1, :], teach[k : k + 1, :], found)
            tgt[pl.ds(first, 64), :] = found

    k = 9
    for off in NEAR:
        slot = z_at(off) * 2 + xl
        a_copy(c, slot, 0, z_peer(off)).wait_recv()
        for peer in (x_peer, core_peer):
            copy = a_copy(c, slot, k, peer)
            copy.start()
            sent.append(copy)
            k += 1
    teacher_work()
    for off in (0, *NEAR):
        slot = z_at(off) * 2 + ox
        a_copy(c, slot, 0, x_peer).wait_recv()
        copy = a_copy(c, slot, k, core_peer)
        copy.start()
        sent.append(copy)
        k += 1
    logits = jnp.dot(wt[c], conv[c].reshape(ZX * CH, T), preferred_element_type=F32)

    @pl.loop(0, ZX)
    def _(slot):
        a_copy(oc, slot, 0, core_peer).wait_recv()

    logits = logits + jnp.dot(wt[oc], conv[oc].reshape(ZX * CH, T), preferred_element_type=F32)

    peak = jnp.max(logits, axis=0, keepdims=True)
    raised = jnp.exp(logits - peak)
    ex[...] = raised
    own = peak + jnp.log(jnp.sum(raised, axis=0, keepdims=True))
    stats[m] = own

    def b_copy(off, slot):
        return remote(
            stats.at[slot], stats.at[slot], b_send.at[off], b_recv.at[slot], {"mp": (m + off) % 32}
        )

    @pl.loop(1, 32)
    def _(off):
        b_copy(off, m).start()

    for copy in sent:
        copy.wait_send()

    @pl.loop(1, 32)
    def _(off):
        b_copy(off, (m + off) % 32).wait_recv()

    every = stats[...]
    most = jnp.max(every, axis=0)
    norm = most + jnp.log(jnp.sum(jnp.exp(every - most[None]), axis=0))
    factor = jnp.exp(peak - norm)
    live = lax.broadcasted_iota(jnp.int32, (1, T), 1) < used[0]
    gt[...] = jnp.where(live, ex[...] * factor - tgt[...], 0.0).astype(BF)

    w_all = w[...].reshape(ZX * 2 * CH, VOC)
    cg[...] = (
        jnp.dot(w_all, gt[...], preferred_element_type=F32).astype(BF).reshape(NZ, 2, 2, CH, T)
    )
    core_copies = []
    for k, side in enumerate((ox, xl)):
        copy = remote(cg.at[:, side, oc], cin.at[k], dc_send.at[k], dc_recv.at[k], core_peer)
        copy.start()
        core_copies.append(copy)

    for half in range(2):
        hh[half] = (
            lax.dot_general(
                conv[half].reshape(ZX * CH, T), gt[...], (((1,), (1,)), ((), ())), preferred_element_type=F32
            )
            .astype(BF)
            .reshape(ZX, CH, VOC)
        )

    def r_copy(way, dist, half, side, owner):
        row = (oh if side == 0 else xh) * NY + owner
        return remote(
            hh.at[half, row],
            rin.at[way, dist - 1, half, side],
            r_send.at[way, dist - 1, half, side],
            r_recv.at[way, dist - 1, half, side],
            y_peer(1 if way else -1),
        )

    def r_step(dist, late):
        for side in range(2):
            for way in range(2):
                toward = dist if way else -dist
                owner = y_at(toward)
                if dist == 4:
                    half = way
                    r_copy(way, dist, half, side, owner).start()
                    continue
                half = way if late else 1 - way
                row = (oh if side == 0 else xh) * NY + owner
                if dist < 3 or late:
                    r_copy(way, dist + 1, half, side, owner).wait_recv()
                    hh[half, row] = (
                        hh[half, row].astype(F32) + rin[way, dist, half, side].astype(F32)
                    ).astype(BF)
                r_copy(way, dist, half, side, owner).start()

    r_step(4, True)
    r_step(3, False)

    def dx_copy(slot):
        return remote(xsend.at[slot], xin.at[slot], dx_send.at[slot], dx_recv.at[slot], x_peer)

    core_copies[0].wait_recv()
    for off in (*FAR, 0):
        at = z_at(off)
        xsend[at] = (cg[at, ox, c].astype(F32) + cin[0, at].astype(F32)).astype(BF)
        dx_copy(at).start()
    core_copies[1].wait_recv()

    def dz_copy(off, slot):
        return remote(zsend.at[slot], zin.at[off], dz_send.at[off], dz_recv.at[off], z_peer(off))

    def d_step(off):
        at = z_at(off)
        dx_copy(at).wait_recv()
        total = cg[at, xl, c].astype(F32) + cin[1, at].astype(F32) + xin[at].astype(F32)
        if off == 0:
            return total
        zsend[at] = total.astype(BF)
        dz_copy(off, at).start()

    for off in FAR[:4]:
        d_step(off)
    r_step(3, True)
    for off in FAR[4:]:
        d_step(off)
    conv_grad = d_step(0)
    r_step(2, False)
    r_step(2, True)
    for off in FAR:
        dz_copy(off, z_at(off)).wait_recv()
        conv_grad = conv_grad + zin[off].astype(F32)

    group = lax.broadcasted_iota(jnp.int32, (1, 8, 128), 2)
    packed = jnp.zeros((2, 8, 128), F32)
    for j in range(TAPS):
        delta = j - LEFT
        terms = moved(xt[...], delta) * only(kept(delta), conv_grad)
        sums = jnp.sum(terms, axis=1, keepdims=True).reshape(CH // 8, 8, 1)
        for g in range(3):
            packed = jnp.where(group == g * TAPS + j, sums[2 * g : 2 * g + 2], packed)
    kg[...] = packed.reshape(16, 128)
    k_over = remote(kg, kx, k_send.at[0], k_recv.at[0], h_peer)
    k_over.start()

    r_step(1, False)

    acc = jnp.zeros((CH, T), F32)
    for j in range(TAPS):
        delta = j - LEFT
        acc = acc + moved(only(kept(delta), conv_grad) * tap_t[:, j : j + 1], -delta)
    out_in[...] = acc

    k_over.wait_recv()
    ky[y] = kg[...] + kx[...]

    def k_copy(off, slot):
        return remote(ky.at[slot], ky.at[slot], k_send.at[off], k_recv.at[slot + 1], y_peer(off))

    for off in range(1, NY):
        k_copy(off, y).start()

    r_step(1, True)

    def cx_copy(half):
        return remote(xfin.at[half], xrin.at[half], cx_send.at[half], cx_recv.at[half], h_peer)

    def y_total(half, side):
        row = (oh if side == 0 else xh) * NY + y
        total = hh[half, row].astype(F32)
        for way in range(2):
            r_copy(way, 1, half, side, y).wait_recv()
            total = total + rin[way, 0, half, side].astype(F32)
        return total

    for half in range(2):
        xfin[half] = y_total(half, 0).astype(BF)
        cx_copy(half).start()

    for off in range(1, NY):
        k_copy(off, y_at(off)).wait_recv()
    out_k[...] = jnp.sum(ky[...], axis=0)

    for half in range(2):
        total = y_total(half, 1)
        cx_copy(half).wait_recv()
        out_h[half] = total + xrin[half].astype(F32)

    @pl.loop(1, 32)
    def _(off):
        b_copy(off, m).wait_send()

    for copy in core_copies:
        copy.wait_send()
    for off in (*FAR, 0):
        dx_copy(z_at(off)).wait_send()
    for off in FAR:
        dz_copy(off, z_at(off)).wait_send()
    for way in range(2):
        for side in range(2):
            r_copy(way, 4, way, side, y).wait_send()
            for dist in range(1, 4):
                for half in range(2):
                    r_copy(way, dist, half, side, y).wait_send()
    for half in range(2):
        cx_copy(half).wait_send()
    k_over.wait_send()
    for off in range(1, NY):
        k_copy(off, y).wait_send()


def local(frames, conv_kernel, head_weight, utterance_ids, tile_used, teacher_ids, teacher_logits, teacher_scale):
    vmem = pl.BlockSpec(memory_space=pltpu.VMEM)
    dma = pltpu.SemaphoreType.DMA
    grad, packed, head = pl.pallas_call(
        kernel,
        out_shape=(
            jax.ShapeDtypeStruct((CH, T), F32),
            jax.ShapeDtypeStruct((16, 128), F32),
            jax.ShapeDtypeStruct((2, CH, VOC), F32),
        ),
        in_specs=[
            vmem,
            vmem,
            pl.BlockSpec(memory_space=pl.ANY),
            vmem,
            pl.BlockSpec(memory_space=pltpu.SMEM),
            vmem,
            vmem,
            vmem,
        ],
        out_specs=(vmem, vmem, vmem),
        scratch_shapes=[
            pltpu.VMEM((ZX, 2, CH, VOC), BF),
            pltpu.VMEM((2, VOC, ZX * CH), BF),
            pltpu.VMEM((2, ZX, CH, T), BF),
            pltpu.VMEM((CH, T), F32),
            pltpu.VMEM((8, T), jnp.int32),
            pltpu.VMEM((8, T), jnp.int32),
            pltpu.VMEM((TOP, T), jnp.int32),
            pltpu.VMEM((TOP, T), F32),
            pltpu.VMEM((VOC, T), F32),
            pltpu.VMEM((VOC, T), F32),
            pltpu.VMEM((32, 1, T), F32),
            pltpu.VMEM((VOC, T), BF),
            pltpu.VMEM((NZ, 2, 2, CH, T), BF),
            pltpu.VMEM((2, NZ, CH, T), BF),
            pltpu.VMEM((NZ, CH, T), BF),
            pltpu.VMEM((NZ, CH, T), BF),
            pltpu.VMEM((NZ, CH, T), BF),
            pltpu.VMEM((NZ, CH, T), BF),
            pltpu.VMEM((2, ZX, CH, VOC), BF),
            pltpu.VMEM((2, 4, 2, 2, CH, VOC), BF),
            pltpu.VMEM((2, CH, VOC), BF),
            pltpu.VMEM((2, CH, VOC), BF),
            pltpu.VMEM((16, 128), F32),
            pltpu.VMEM((16, 128), F32),
            pltpu.VMEM((NY, 16, 128), F32),
            dma,
            dma((32,)),
            dma((2, ZX)),
            dma((32,)),
            dma((32,)),
            dma((2,)),
            dma((2,)),
            dma((NZ,)),
            dma((NZ,)),
            dma((NZ,)),
            dma((NZ,)),
            dma((2, 4, 2, 2)),
            dma((2, 4, 2, 2)),
            dma((2,)),
            dma((2,)),
            dma((NY,)),
            dma((NY + 1,)),
        ],
        compiler_params=pltpu.CompilerParams(
            collective_id=0, has_side_effects=True, vmem_limit_bytes=56 * 1024 * 1024
        ),
    )(
        frames,
        conv_kernel,
        head_weight.reshape(ZX, 2, CH, VOC),
        utterance_ids,
        tile_used,
        teacher_ids,
        teacher_logits,
        teacher_scale,
    )
    kernel_grad = packed[:, : 3 * TAPS].reshape(16, 3, TAPS).transpose(2, 1, 0).reshape(TAPS, CH)
    return grad.T, kernel_grad, head.reshape(2 * CH, VOC)


def solution(mesh):
    return jax.shard_map(
        local,
        mesh=mesh,
        in_specs=(
            P("dp", "mp"),
            P(None, "mp"),
            P(None, "mp"),
            P("dp", None),
            P("dp"),
            P("dp", None),
            P("dp", None),
            P("dp"),
        ),
        out_specs=(P("dp", "mp"), P(None, "mp"), P("dp", "mp")),
        check_vma=False,
    )
```

time: 199 us -> 73.9 us (0.37)
  the two profiles are of different devices: /device:TPU:1 before, /device:TPU:24 now
where the time goes in v1:
time: 73.9 us; the launch traced here: 73.5 us
  Pallas kernels  63.2 us (86%)
  local copies, waits for them, and re-layouts  8.97 us (12%)
  between operations  1.29 us (2%)
    pallas_call x1, Pallas kernels, local(): pl.pallas_call(kernel, out_shape=(jax.ShapeDtypeStruct((CH, T), F32), jax...  63.2 us
    unnamed x6, local copies, waits for them, and re-layouts  8.19 us

profile of v1, /device:TPU:24, one launch (start us, length us, event | category | flops | bytes accessed | tf_op | source)
XLA Modules:
  0.0 73.5 jit_solution(14412526425898225368)
XLA Ops:
  1.3 1.5 %copy.15.frames = bf16[256,48]{1,0:T(8,128)(2,1)} copy(bf16[256,48]{0,1:T(8,128)(2,1)} %param.8) | data formatting | bytes 49152 | tf_op args[0]
  2.7 1.5 %copy.16.ids = s32[256,32]{1,0:T(8,128)} copy(s32[256,32]{0,1:T(8,128)} %param.13) | data formatting | bytes 65536 | tf_op args[5]
  4.2 1.5 %copy.17.tlog = s32[256,32]{1,0:T(8,128)} copy(s32[256,32]{0,1:T(8,128)} %param.14) | data formatting | bytes 65536 | tf_op args[6]
  5.7 63.2 %shard_map.103 = (f32[48,256]{1,0:T(8,128)}, f32[16,128]{1,0:T(8,128)}, f32[2,48,512]{2,1,0:T(8,128)}) custom-call(bf16[256,48]{1,0:T(8,128)(2,1)} %copy.15.frames, bf16[32,48]{1,0:T(8,128)(2,1)} %taps.1, bf16[16,2,48,512]{3,2,1,0:T(8,128)(2,1)} %bitcast.6, s32[1,256]{1,0:T(1,128)} %seg.1, s32[1]{0:T(128)S(6)} %copy.22.used, s32[256,32]{1,0:T(8,128)} %copy.16.ids, ...), custom_call_target="tpu_custom_call" | custom-call | tf_op jit(solution)/shard_map/pallas_call | solution.py:379
  69.0 0.8 %reshape.19 = f32[16,3,32]{2,1,0:T(4,128)S(1)} reshape(f32[16,96]{1,0:T(8,128)} %bitcast.11) | data formatting | bytes 12288 | tf_op jit(solution)/shard_map/reshape | solution.py:454
  69.8 0.7 copy.19
  70.4 1.4 %copy.23 = f32[256,48]{0,1:T(8,128)} copy(f32[256,48]{0,1:T(8,128)} %bitcast.10) | data formatting | bytes 98304
  71.9 1.6 %copy.24 = f32[96,512]{1,0:T(8,128)} copy(f32[96,512]{1,0:T(8,128)} %bitcast.7) | data formatting | bytes 393216
  (1 shorter events, 0.0 us)

commit v2 on v1

v2 whole, which is shorter than its diff:
```python
import jax
import jax.numpy as jnp
from jax import lax
from jax.experimental import pallas as pl
from jax.experimental.pallas import tpu as pltpu
from jax.sharding import PartitionSpec as P

MESH = pl.DeviceIdType.MESH
TAPS = 32
LEFT = (TAPS - 1) // 2
TOP = 32
NZ = 8
NY = 8
CH = 48
T = 256
VOC = 512
ZX = 16
F32 = jnp.float32
BF = jnp.bfloat16

NEAR = (1, 7, 2, 6, 3, 5, 4)
FAR = (4, 3, 5, 2, 6, 1, 7)
SENDS = (4, 1, 7, 2, 6, 3, 5)


def eye(n):
    same = lax.broadcasted_iota(jnp.int32, (n, n), 0) == lax.broadcasted_iota(jnp.int32, (n, n), 1)
    return jnp.where(same, 1.0, 0.0).astype(BF)


def turned(values):
    return lax.dot_general(
        eye(values.shape[1]), values, (((1,), (1,)), ((), ())), preferred_element_type=F32
    )


def kernel(
    used, frames_hbm, taps_hbm, w_hbm, seg_hbm, ids_hbm, tlog_hbm, scale_hbm,
    out_in, out_k, out_h,
    frames, taps, seg, ids, tlog, scale,
    w, wt, conv, xt, xm, src_rows, dst_rows, rel_ids, teach, tgt, ex, stats, gt,
    cg, cin, xsend, xin, zsend, zin, grad,
    hh, rin, xfin, xrin, ky,
    in_sem, a_send, a_recv, b_send, b_recv, dc_send, dc_recv, dx_send, dx_recv, dz_send, dz_recv,
    r_send, r_recv, cx_send, cx_recv, k_send, k_recv,
):
    m = lax.axis_index("mp")
    d = lax.axis_index("dp")
    c, xl, z = m % 2, (m // 2) % 2, m // 4
    y, xh = d % NY, d // NY
    zx = m // 2
    oc, ox, oh = 1 - c, 1 - xl, 1 - xh
    core_peer = {"mp": m + 1 - 2 * c}
    x_peer = {"mp": m + 2 - 4 * xl}
    h_peer = {"dp": oh * NY + y}

    def z_at(off):
        return (z + off) % NZ

    def z_peer(off):
        return {"mp": z_at(off) * 4 + xl * 2 + c}

    def y_at(off):
        return (y + off + NY) % NY

    def y_peer(off):
        return {"dp": xh * NY + y_at(off)}

    pairs = (
        (frames_hbm, frames), (taps_hbm, taps), (seg_hbm, seg),
        (w_hbm, w), (ids_hbm, ids), (tlog_hbm, tlog), (scale_hbm, scale),
    )
    loads = [pltpu.make_async_copy(src, dst, in_sem.at[k]) for k, (src, dst) in enumerate(pairs)]
    for load in loads:
        load.start()

    barrier = pltpu.get_barrier_semaphore()

    @pl.loop(1, 32)
    def _(off):
        pl.semaphore_signal(barrier, inc=1, device_id={"mp": (m + off) % 32}, device_id_type=MESH)

    @pl.loop(1, 16)
    def _(off):
        pl.semaphore_signal(barrier, inc=1, device_id={"dp": (d + off) % 16}, device_id_type=MESH)

    def remote(src, dst, send, recv, peer):
        return pltpu.make_async_remote_copy(
            src_ref=src, dst_ref=dst, send_sem=send, recv_sem=recv, device_id=peer, device_id_type=MESH
        )

    for load in loads[:3]:
        load.wait()

    lane = lax.broadcasted_iota(jnp.int32, (8, T), 1)
    valid = lane < used[0]
    seg_rows = jnp.broadcast_to(seg[...], (8, T))
    src_rows[...] = jnp.where(valid, seg_rows, -1)
    dst_rows[...] = jnp.where(valid, seg_rows, -2)
    xt[...] = frames[...].astype(F32)
    tap_t = turned(taps[...])

    def kept(delta):
        rolled = src_rows[...]
        if delta:
            rolled = pltpu.roll(rolled, (-delta) % T, 1)
        keep = rolled == dst_rows[...]
        if delta > 0:
            keep = keep & (lane < T - delta)
        if delta < 0:
            keep = keep & (lane >= -delta)
        return keep

    def moved(values, delta):
        return pltpu.roll(values, (-delta) % T, 1) if delta else values

    def only(keep, values):
        return jnp.where(keep[None], values.reshape(CH // 8, 8, T), 0.0).reshape(CH, T)

    acc = jnp.zeros((CH, T), F32)
    for j in range(TAPS):
        delta = j - LEFT
        source = only(kept(delta), moved(xt[...], delta))
        xm[j] = source
        acc = acc + source * tap_t[:, j : j + 1]
    conv[c, zx] = acc.astype(BF)

    pl.semaphore_wait(barrier, 31 + 15)

    def a_copy(slot_c, slot_zx, k, peer):
        return remote(
            conv.at[slot_c, slot_zx], conv.at[slot_c, slot_zx], a_send.at[k], a_recv.at[slot_c, slot_zx], peer
        )

    sent = []

    def a_start(slot, peer):
        copy = a_copy(c, slot, len(sent), peer)
        copy.start()
        sent.append(copy)

    a_start(zx, x_peer)
    a_start(zx, core_peer)
    for off in SENDS:
        a_start(zx, z_peer(off))

    for load in loads[3:]:
        load.wait()
    for half in range(2):
        for v in range(VOC // 128):
            part = w[:, :, half, :, v * 128 : (v + 1) * 128].reshape(ZX * CH, 128)
            wt[half, v * 128 : (v + 1) * 128, :] = part.T

    rel_ids[...] = ids[...] - m * VOC
    scores = scale[...].reshape(1, T) * tlog[...].astype(F32)
    top = jnp.exp(scores - jnp.max(scores, axis=0, keepdims=True))
    teach[...] = top / jnp.sum(top, axis=0, keepdims=True)

    @pl.loop(0, VOC // 64)
    def _(part):
        first = pl.multiple_of(part * 64, 64)
        row = lax.broadcasted_iota(jnp.int32, (64, T), 0) + first
        found = jnp.zeros((64, T), F32)
        for k in range(TOP):
            found = jnp.where(row == rel_ids[k : k + 1, :], teach[k : k + 1, :], found)
        tgt[pl.ds(first, 64), :] = found

    def over(off):
        slot = z_at(off) * 2 + ox
        a_copy(c, slot, 0, x_peer).wait_recv()
        a_start(slot, core_peer)

    over(0)
    for off in NEAR:
        slot = z_at(off) * 2 + xl
        a_copy(c, slot, 0, z_peer(off)).wait_recv()
        a_start(slot, x_peer)
        a_start(slot, core_peer)
    for off in NEAR:
        over(off)
    logits = jnp.dot(wt[c], conv[c].reshape(ZX * CH, T), preferred_element_type=F32)

    @pl.loop(0, ZX)
    def _(slot):
        a_copy(oc, slot, 0, core_peer).wait_recv()

    logits = logits + jnp.dot(wt[oc], conv[oc].reshape(ZX * CH, T), preferred_element_type=F32)

    peak = jnp.max(logits, axis=0, keepdims=True)
    raised = jnp.exp(logits - peak)
    ex[...] = raised
    own = peak + jnp.log(jnp.sum(raised, axis=0, keepdims=True))
    stats[m] = own

    def b_copy(off, slot):
        return remote(
            stats.at[slot], stats.at[slot], b_send.at[off], b_recv.at[slot], {"mp": (m + off) % 32}
        )

    @pl.loop(1, 32)
    def _(off):
        b_copy(off, m).start()

    for copy in sent:
        copy.wait_send()

    @pl.loop(1, 32)
    def _(off):
        b_copy(off, (m + off) % 32).wait_recv()

    every = stats[...]
    most = jnp.max(every, axis=0)
    norm = most + jnp.log(jnp.sum(jnp.exp(every - most[None]), axis=0))
    factor = jnp.exp(peak - norm)
    live = lax.broadcasted_iota(jnp.int32, (1, T), 1) < used[0]
    gt[...] = jnp.where(live, ex[...] * factor - tgt[...], 0.0).astype(BF)

    core_copies = []
    for k, (side, core) in enumerate(((ox, oc), (xl, oc), (ox, c), (xl, c))):
        rows = w[:, side, core].reshape(NZ * CH, VOC)
        cg[k] = jnp.dot(rows, gt[...], preferred_element_type=F32).astype(BF).reshape(NZ, CH, T)
        if k < 2:
            copy = remote(cg.at[k], cin.at[k], dc_send.at[k], dc_recv.at[k], core_peer)
            copy.start()
            core_copies.append(copy)

    for half in range(2):
        for col in range(2):
            hh[half, col] = (
                lax.dot_general(
                    conv[half].reshape(ZX * CH, T),
                    gt[col * T : (col + 1) * T, :],
                    (((1,), (1,)), ((), ())),
                    preferred_element_type=F32,
                )
                .astype(BF)
                .reshape(ZX, CH, T)
            )

    def row_of(side, owner):
        return (oh if side == 0 else xh) * NY + owner

    def r_copy(way, dist, half, side, col, owner):
        at = (way, dist - 1, half, side, col)
        return remote(
            hh.at[half, col, row_of(side, owner)], rin.at[at], r_send.at[at], r_recv.at[at], y_peer(1 if way else -1)
        )

    def r_step(dist, late):
        for side in range(2):
            for col in range(2):
                for way in range(2):
                    owner = y_at(dist if way else -dist)
                    if dist == 4:
                        r_copy(way, dist, way, side, col, owner).start()
                        continue
                    half = way if late else 1 - way
                    if dist < 3 or late:
                        row = row_of(side, owner)
                        r_copy(way, dist + 1, half, side, col, owner).wait_recv()
                        hh[half, col, row] = (
                            hh[half, col, row].astype(F32) + rin[way, dist, half, side, col].astype(F32)
                        ).astype(BF)
                    r_copy(way, dist, half, side, col, owner).start()

    r_step(4, True)

    def dx_copy(slot):
        return remote(xsend.at[slot], xin.at[slot], dx_send.at[slot], dx_recv.at[slot], x_peer)

    core_copies[0].wait_recv()
    for off in (*FAR, 0):
        at = z_at(off)
        xsend[at] = (cg[2, at].astype(F32) + cin[0, at].astype(F32)).astype(BF)
        dx_copy(at).start()
    core_copies[1].wait_recv()

    def dz_copy(off, slot):
        return remote(zsend.at[slot], zin.at[off], dz_send.at[off], dz_recv.at[off], z_peer(off))

    def d_step(off):
        at = z_at(off)
        dx_copy(at).wait_recv()
        total = cg[3, at].astype(F32) + cin[1, at].astype(F32) + xin[at].astype(F32)
        if off == 0:
            grad[...] = total
            return
        zsend[at] = total.astype(BF)
        dz_copy(off, at).start()

    for side in range(2):
        for col in range(2):
            for way in range(2):
                r_copy(way, 4, way, side, col, y).wait_send()
    r_step(3, False)

    @pl.loop(1, 32)
    def _(off):
        b_copy(off, m).wait_send()

    for copy in core_copies:
        copy.wait_send()
    r_step(3, True)
    for off in (*FAR, 0):
        d_step(off)
    for off in (*FAR, 0):
        dx_copy(z_at(off)).wait_send()
    r_step(2, False)
    r_step(2, True)
    r_step(1, False)
    r_step(1, True)
    conv_grad = grad[...]
    for off in FAR:
        dz_copy(off, z_at(off)).wait_recv()
        conv_grad = conv_grad + zin[off].astype(F32)
    grad[...] = conv_grad

    group = lax.broadcasted_iota(jnp.int32, (1, 8, 128), 2)

    def k_terms(some, packed):
        for j in some:
            terms = xm[j] * grad[...]
            sums = jnp.sum(terms[:, :128] + terms[:, 128:], axis=1, keepdims=True).reshape(CH // 8, 8, 1)
            for g in range(3):
                packed = jnp.where(group == g * TAPS + j, sums[2 * g : 2 * g + 2], packed)
        return packed

    packed = k_terms(range(TAPS), jnp.zeros((2, 8, 128), F32))
    ky[d] = packed.reshape(16, 128)

    def k_copy(off, slot):
        return remote(ky.at[slot], ky.at[slot], k_send.at[off], k_recv.at[slot], {"dp": (d + off) % 16})

    @pl.loop(1, 16)
    def _(off):
        k_copy(off, d).start()

    def cx_copy(half, col):
        return remote(xfin.at[half, col], xrin.at[half, col], cx_send.at[half, col], cx_recv.at[half, col], h_peer)

    def y_total(half, col, side):
        total = hh[half, col, row_of(side, y)].astype(F32)
        for way in range(2):
            r_copy(way, 1, half, side, col, y).wait_recv()
            total = total + rin[way, 0, half, side, col].astype(F32)
        return total

    for half in range(2):
        for col in range(2):
            xfin[half, col] = y_total(half, col, 0).astype(BF)
            cx_copy(half, col).start()

    acc = jnp.zeros((CH, T), F32)
    for j in range(TAPS):
        delta = j - LEFT
        acc = acc + only(kept(-delta), moved(grad[...], -delta) * tap_t[:, j : j + 1])
    out_in[...] = acc

    for half in range(2):
        for col in range(2):
            out_h[half, :, col * T : (col + 1) * T] = y_total(half, col, 1)

    for off in FAR:
        dz_copy(off, z_at(off)).wait_send()
    for way in range(2):
        for side in range(2):
            for col in range(2):
                for dist in range(1, 4):
                    for half in range(2):
                        r_copy(way, dist, half, side, col, y).wait_send()

    @pl.loop(1, 16)
    def _(off):
        k_copy(off, d).wait_send()

    @pl.loop(1, 16)
    def _(off):
        k_copy(off, (d + off) % 16).wait_recv()

    flat = jnp.sum(ky[...], axis=0).T
    out_k[...] = jnp.concatenate([flat[g * TAPS : (g + 1) * TAPS, :] for g in range(3)], axis=1)

    for half in range(2):
        for col in range(2):
            cx_copy(half, col).wait_recv()
            cols = slice(col * T, (col + 1) * T)
            out_h[half, :, cols] = out_h[half, :, cols] + xrin[half, col].astype(F32)

    for half in range(2):
        for col in range(2):
            cx_copy(half, col).wait_send()


def put_out(a, b, c, out_a, out_b, out_c, sem):
    copies = [
        pltpu.make_async_copy(src, dst, sem.at[k]) for k, (src, dst) in enumerate(((c, out_c), (a, out_a), (b, out_b)))
    ]
    for copy in copies:
        copy.start()
    for copy in copies:
        copy.wait()


def local(frames, conv_kernel, head_weight, utterance_ids, tile_used, teacher_ids, teacher_logits, teacher_scale):
    vmem = pl.BlockSpec(memory_space=pltpu.VMEM)
    anywhere = pl.BlockSpec(memory_space=pl.ANY)
    dma = pltpu.SemaphoreType.DMA
    shapes = (
        jax.ShapeDtypeStruct((CH, T), F32),
        jax.ShapeDtypeStruct((TAPS, CH), F32),
        jax.ShapeDtypeStruct((2, CH, VOC), F32),
    )
    given = (
        frames.T,
        conv_kernel,
        head_weight.reshape(NZ, 2, 2, CH, VOC),
        utterance_ids,
        teacher_ids.T,
        teacher_logits.T,
        teacher_scale,
    )
    results = pl.pallas_call(
        kernel,
        out_shape=shapes,
        in_specs=[pl.BlockSpec(memory_space=pltpu.SMEM)] + [anywhere] * 7,
        out_specs=(vmem, vmem, vmem),
        scratch_shapes=[
            pltpu.VMEM((CH, T), BF),
            pltpu.VMEM((TAPS, CH), BF),
            pltpu.VMEM((1, T), jnp.int32),
            pltpu.VMEM((TOP, T), jnp.int32),
            pltpu.VMEM((TOP, T), jnp.int32),
            pltpu.VMEM((T,), F32),
            pltpu.VMEM((NZ, 2, 2, CH, VOC), BF),
            pltpu.VMEM((2, VOC, ZX * CH), BF),
            pltpu.VMEM((2, ZX, CH, T), BF),
            pltpu.VMEM((CH, T), F32),
            pltpu.VMEM((TAPS, CH, T), F32),
            pltpu.VMEM((8, T), jnp.int32),
            pltpu.VMEM((8, T), jnp.int32),
            pltpu.VMEM((TOP, T), jnp.int32),
            pltpu.VMEM((TOP, T), F32),
            pltpu.VMEM((VOC, T), F32),
            pltpu.VMEM((VOC, T), F32),
            pltpu.VMEM((32, 1, T), F32),
            pltpu.VMEM((VOC, T), BF),
            pltpu.VMEM((4, NZ, CH, T), BF),
            pltpu.VMEM((2, NZ, CH, T), BF),
            pltpu.VMEM((NZ, CH, T), BF),
            pltpu.VMEM((NZ, CH, T), BF),
            pltpu.VMEM((NZ, CH, T), BF),
            pltpu.VMEM((NZ, CH, T), BF),
            pltpu.VMEM((CH, T), F32),
            pltpu.VMEM((2, 2, ZX, CH, T), BF),
            pltpu.VMEM((2, 4, 2, 2, 2, CH, T), BF),
            pltpu.VMEM((2, 2, CH, T), BF),
            pltpu.VMEM((2, 2, CH, T), BF),
            pltpu.VMEM((16, 16, 128), F32),
            dma((7,)),
            dma((31,)),
            dma((2, ZX)),
            dma((32,)),
            dma((32,)),
            dma((2,)),
            dma((2,)),
            dma((NZ,)),
            dma((NZ,)),
            dma((NZ,)),
            dma((NZ,)),
            dma((2, 4, 2, 2, 2)),
            dma((2, 4, 2, 2, 2)),
            dma((2, 2)),
            dma((2, 2)),
            dma((16,)),
            dma((16,)),
        ],
        compiler_params=pltpu.CompilerParams(
            collective_id=0, has_side_effects=True, vmem_limit_bytes=24 * 1024 * 1024
        ),
    )(
        tile_used, *(pltpu.with_memory_space_constraint(value, pltpu.HBM) for value in given)
    )
    grad, kernel_grad, head = pl.pallas_call(
        put_out,
        out_shape=shapes,
        in_specs=[vmem] * 3,
        out_specs=(anywhere,) * 3,
        scratch_shapes=[dma((3,))],
        compiler_params=pltpu.CompilerParams(vmem_limit_bytes=4 * 1024 * 1024),
    )(*results)
    return grad.T, kernel_grad, head.reshape(2 * CH, VOC)


def solution(mesh):
    return jax.shard_map(
        local,
        mesh=mesh,
        in_specs=(
            P("dp", "mp"),
            P(None, "mp"),
            P(None, "mp"),
            P("dp", None),
            P("dp"),
            P("dp", None),
            P("dp", None),
            P("dp"),
        ),
        out_specs=(P("dp", "mp"), P(None, "mp"), P("dp", "mp")),
        check_vma=False,
    )
```

time: 73.9 us -> 61.1 us (0.83)
  the two profiles are of different devices: /device:TPU:24 before, /device:TPU:1 now
where the time goes in v2:
time: 61.1 us; the launch traced here: 61 us
  Pallas kernels  59.7 us (98%)
  between operations  1.29 us (2%)
    pallas_call x1, Pallas kernels, local(): pl.pallas_call(kernel, out_shape=shapes, in_specs=[pl.BlockSpec(memory_sp...  59 us

profile of v2, /device:TPU:1, one launch (start us, length us, event | category | flops | bytes accessed | tf_op | source)
XLA Modules:
  0.0 61.0 jit_solution(6408316015529474691)
XLA Ops:
  1.3 59.0 %shard_map.103 = (f32[48,256]{1,0:T(8,128)S(1)}, f32[32,48]{1,0:T(8,128)S(1)}, f32[2,48,512]{2,1,0:T(8,128)S(1)}) custom-call(s32[1]{0:T(128)S(6)} %copy.11.used, bf16[48,256]{1,0:T(8,128)(2,1)} %bitcast.9, bf16[32,48]{1,0:T(8,128)(2,1)} %taps_hbm.1, bf16[8,2,2,48,512]{4,3,2,1,0:T(8,128)(2,1)} %bitcast.6, s32[1,256]{1,0:T(1,128)} %seg_hbm.1, ...), custom_call_target="tpu_custom_call" | custom-call | tf_op jit(solution)/shard_map/pallas_call | solution.py:422
  60.3 0.7 %shard_map.104 = (f32[48,256]{1,0:T(8,128)}, f32[32,48]{1,0:T(8,128)}, f32[2,48,512]{2,1,0:T(8,128)}) custom-call(f32[48,256]{1,0:T(8,128)S(1)} %get-tuple-element.9.a, f32[32,48]{1,0:T(8,128)S(1)} %get-tuple-element.10.b, f32[2,48,512]{2,1,0:T(8,128)S(1)} %get-tuple-element.11.c), custom_call_target="tpu_custom_call" | custom-call | tf_op jit(solution)/shard_map/pallas_call | solution.py:483

commit v3 on v2

--- a/solution.py
+++ b/solution.py
@@ -39,10 +39,10 @@
     out_in, out_k, out_h,
     frames, taps, seg, ids, tlog, scale,
     w, wt, conv, xt, xm, src_rows, dst_rows, rel_ids, teach, tgt, ex, stats, gt,
-    cg, cin, xsend, xin, zsend, zin, grad,
-    hh, rin, xfin, xrin, ky,
-    in_sem, a_send, a_recv, b_send, b_recv, dc_send, dc_recv, dx_send, dx_recv, dz_send, dz_recv,
-    r_send, r_recv, cx_send, cx_recv, k_send, k_recv,
+    cg, cin, zsend, zin, grad,
+    h4, hh, rin, xrin, ky,
+    in_sem, a_send, a_recv, b_send, b_recv, dc_send, dc_recv, dz_send, dz_recv,
+    r_send, r_recv, cx_send, cx_recv, k_send, k_recv, column_sem,
 ):
     m = lax.axis_index("mp")
     d = lax.axis_index("dp")
@@ -76,13 +76,9 @@
 
     barrier = pltpu.get_barrier_semaphore()
 
-    @pl.loop(1, 32)
-    def _(off):
-        pl.semaphore_signal(barrier, inc=1, device_id={"mp": (m + off) % 32}, device_id_type=MESH)
-
-    @pl.loop(1, 16)
-    def _(off):
-        pl.semaphore_signal(barrier, inc=1, device_id={"dp": (d + off) % 16}, device_id_type=MESH)
+    near = [z_peer(off) for off in FAR] + [y_peer(off) for off in FAR] + [x_peer, core_peer, h_peer]
+    for peer in near:
+        pl.semaphore_signal(barrier, inc=1, device_id=peer, device_id_type=MESH)
 
     def remote(src, dst, send, recv, peer):
         return pltpu.make_async_remote_copy(
@@ -125,7 +121,8 @@
         acc = acc + source * tap_t[:, j : j + 1]
     conv[c, zx] = acc.astype(BF)
 
-    pl.semaphore_wait(barrier, 31 + 15)
+    pl.semaphore_wait(barrier, len(near))
+    pl.semaphore_signal(column_sem, inc=1, device_id=h_peer, device_id_type=MESH)
 
     def a_copy(slot_c, slot_zx, k, peer):
         return remote(
@@ -215,36 +212,16 @@
     live = lax.broadcasted_iota(jnp.int32, (1, T), 1) < used[0]
     gt[...] = jnp.where(live, ex[...] * factor - tgt[...], 0.0).astype(BF)
 
-    core_copies = []
-    for k, (side, core) in enumerate(((ox, oc), (xl, oc), (ox, c), (xl, c))):
-        rows = w[:, side, core].reshape(NZ * CH, VOC)
-        cg[k] = jnp.dot(rows, gt[...], preferred_element_type=F32).astype(BF).reshape(NZ, CH, T)
-        if k < 2:
-            copy = remote(cg.at[k], cin.at[k], dc_send.at[k], dc_recv.at[k], core_peer)
-            copy.start()
-            core_copies.append(copy)
-
-    for half in range(2):
-        for col in range(2):
-            hh[half, col] = (
-                lax.dot_general(
-                    conv[half].reshape(ZX * CH, T),
-                    gt[col * T : (col + 1) * T, :],
-                    (((1,), (1,)), ((), ())),
-                    preferred_element_type=F32,
-                )
-                .astype(BF)
-                .reshape(ZX, CH, T)
-            )
-
     def row_of(side, owner):
         return (oh if side == 0 else xh) * NY + owner
 
     def r_copy(way, dist, half, side, col, owner):
         at = (way, dist - 1, half, side, col)
-        return remote(
-            hh.at[half, col, row_of(side, owner)], rin.at[at], r_send.at[at], r_recv.at[at], y_peer(1 if way else -1)
-        )
+        peer = y_peer(1 if way else -1)
+        if dist == 1 and side == 0:
+            peer = {"dp": oh * NY + y_at(1 if way else -1)}
+        src = h4.at[half, side, col] if dist == 4 else hh.at[half, col, row_of(side, owner)]
+        return remote(src, rin.at[at], r_send.at[at], r_recv.at[at], peer)
 
     def r_step(dist, late):
         for side in range(2):
@@ -263,36 +240,60 @@
                         ).astype(BF)
                     r_copy(way, dist, half, side, col, owner).start()
 
+    spots = [(half, side) for half in range(2) for side in range(2)]
+    rows = jnp.concatenate([conv[half, row_of(side, y_at(4))] for half, side in spots])
+    for col in range(2):
+        part = lax.dot_general(
+            rows, gt[col * T : (col + 1) * T, :], (((1,), (1,)), ((), ())), preferred_element_type=F32
+        ).astype(BF)
+        for k, (half, side) in enumerate(spots):
+            h4[half, side, col] = part[k * CH : (k + 1) * CH]
     r_step(4, True)
 
-    def dx_copy(slot):
-        return remote(xsend.at[slot], xin.at[slot], dx_send.at[slot], dx_recv.at[slot], x_peer)
-
+    core_copies = []
+    for core in (oc, c):
+        rows = jnp.concatenate([w[:, side, core].reshape(NZ * CH, VOC) for side in (ox, xl)])
+        terms = jnp.dot(rows, gt[...], preferred_element_type=F32).astype(BF)
+        for side in range(2):
+            k = side if core is oc else side + 2
+            cg[k] = terms[side * NZ * CH : (side + 1) * NZ * CH].reshape(NZ, CH, T)
+            if k < 2:
+                copy = remote(cg.at[k], cin.at[k], dc_send.at[k], dc_recv.at[k], core_peer)
+                copy.start()
+                core_copies.append(copy)
+
+    def d_copy(i, off):
+        peer = {"mp": z_at(off) * 4 + (xl if i else ox) * 2 + c}
+        return remote(zsend.at[i, off], zin.at[i, off], dz_send.at[i, off], dz_recv.at[i, off], peer)
+
+    d_moves = [(i, off) for i in range(2) for off in (*FAR, 0) if (i, off) != (1, 0)]
     core_copies[0].wait_recv()
-    for off in (*FAR, 0):
+    for i, off in d_moves:
+        if (i, off) == (1, FAR[0]):
+            core_copies[1].wait_recv()
         at = z_at(off)
-        xsend[at] = (cg[2, at].astype(F32) + cin[0, at].astype(F32)).astype(BF)
-        dx_copy(at).start()
-    core_copies[1].wait_recv()
-
-    def dz_copy(off, slot):
-        return remote(zsend.at[slot], zin.at[off], dz_send.at[off], dz_recv.at[off], z_peer(off))
-
-    def d_step(off):
-        at = z_at(off)
-        dx_copy(at).wait_recv()
-        total = cg[3, at].astype(F32) + cin[1, at].astype(F32) + xin[at].astype(F32)
-        if off == 0:
-            grad[...] = total
-            return
-        zsend[at] = total.astype(BF)
-        dz_copy(off, at).start()
-
+        zsend[i, off] = (cg[2 + i, at].astype(F32) + cin[i, at].astype(F32)).astype(BF)
+        d_copy(i, off).start()
+    grad[...] = cg[3, z].astype(F32) + cin[1, z].astype(F32)
+
+    for half in range(2):
+        for col in range(2):
+            hh[half, col] = (
+                lax.dot_general(
+                    conv[half].reshape(ZX * CH, T),
+                    gt[col * T : (col + 1) * T, :],
+                    (((1,), (1,)), ((), ())),
+                    preferred_element_type=F32,
+                )
+                .astype(BF)
+                .reshape(ZX, CH, T)
+            )
+
+    r_step(3, False)
     for side in range(2):
         for col in range(2):
             for way in range(2):
                 r_copy(way, 4, way, side, col, y).wait_send()
-    r_step(3, False)
 
     @pl.loop(1, 32)
     def _(off):
@@ -301,32 +302,37 @@
     for copy in core_copies:
         copy.wait_send()
     r_step(3, True)
-    for off in (*FAR, 0):
-        d_step(off)
-    for off in (*FAR, 0):
-        dx_copy(z_at(off)).wait_send()
     r_step(2, False)
     r_step(2, True)
+
+    def cx_copy(half, col):
+        return remote(
+            hh.at[half, col, row_of(0, y)],
+            xrin.at[half, col],
+            cx_send.at[half, col],
+            cx_recv.at[half, col],
+            h_peer,
+        )
+
+    for half in range(2):
+        for col in range(2):
+            cx_copy(half, col).start()
+    pl.semaphore_wait(column_sem, 1)
     r_step(1, False)
-    r_step(1, True)
     conv_grad = grad[...]
-    for off in FAR:
-        dz_copy(off, z_at(off)).wait_recv()
-        conv_grad = conv_grad + zin[off].astype(F32)
+    for i, off in d_moves:
+        d_copy(i, off).wait_recv()
+        conv_grad = conv_grad + zin[i, off].astype(F32)
     grad[...] = conv_grad
 
     group = lax.broadcasted_iota(jnp.int32, (1, 8, 128), 2)
-
-    def k_terms(some, packed):
-        for j in some:
-            terms = xm[j] * grad[...]
-            sums = jnp.sum(terms[:, :128] + terms[:, 128:], axis=1, keepdims=True).reshape(CH // 8, 8, 1)
-            for g in range(3):
-                packed = jnp.where(group == g * TAPS + j, sums[2 * g : 2 * g + 2], packed)
-        return packed
-
-    packed = k_terms(range(TAPS), jnp.zeros((2, 8, 128), F32))
-    ky[d] = packed.reshape(16, 128)
+    packed = jnp.zeros((2, 8, 128), F32)
+    for j in range(TAPS):
+        terms = xm[j] * grad[...]
+        sums = jnp.sum(terms[:, :128] + terms[:, 128:], axis=1, keepdims=True).reshape(CH // 8, 8, 1)
+        for g in range(3):
+            packed = jnp.where(group == g * TAPS + j, sums[2 * g : 2 * g + 2], packed)
+    ky[d] = packed.reshape(16, 128).astype(BF)
 
     def k_copy(off, slot):
         return remote(ky.at[slot], ky.at[slot], k_send.at[off], k_recv.at[slot], {"dp": (d + off) % 16})
@@ -335,20 +341,7 @@
     def _(off):
         k_copy(off, d).start()
 
-    def cx_copy(half, col):
-        return remote(xfin.at[half, col], xrin.at[half, col], cx_send.at[half, col], cx_recv.at[half, col], h_peer)
-
-    def y_total(half, col, side):
-        total = hh[half, col, row_of(side, y)].astype(F32)
-        for way in range(2):
-            r_copy(way, 1, half, side, col, y).wait_recv()
-            total = total + rin[way, 0, half, side, col].astype(F32)
-        return total
-
-    for half in range(2):
-        for col in range(2):
-            xfin[half, col] = y_total(half, col, 0).astype(BF)
-            cx_copy(half, col).start()
+    r_step(1, True)
 
     acc = jnp.zeros((CH, T), F32)
     for j in range(TAPS):
@@ -356,39 +349,55 @@
         acc = acc + only(kept(-delta), moved(grad[...], -delta) * tap_t[:, j : j + 1])
     out_in[...] = acc
 
-    for half in range(2):
-        for col in range(2):
-            out_h[half, :, col * T : (col + 1) * T] = y_total(half, col, 1)
-
-    for off in FAR:
-        dz_copy(off, z_at(off)).wait_send()
+    for i, off in d_moves:
+        d_copy(i, off).wait_send()
     for way in range(2):
         for side in range(2):
             for col in range(2):
-                for dist in range(1, 4):
+                for dist in range(2, 4):
                     for half in range(2):
                         r_copy(way, dist, half, side, col, y).wait_send()
+    for half in range(2):
+        for col in range(2):
+            cx_copy(half, col).wait_send()
+
+    def y_total(half, col, total, sides):
+        for side in sides:
+            for way in range(2):
+                r_copy(way, 1, half, side, col, y).wait_recv()
+                total = total + rin[way, 0, half, side, col].astype(F32)
+        return total
+
+    for half in range(2):
+        for col in range(2):
+            cx_copy(half, col).wait_recv()
+
+    for half in range(2):
+        for col in range(2):
+            total = hh[half, col, row_of(1, y)].astype(F32) + xrin[half, col].astype(F32)
+            out_h[half, :, col * T : (col + 1) * T] = y_total(half, col, total, (1,))
+
+    @pl.loop(1, 16)
+    def _(off):
+        k_copy(off, (d + off) % 16).wait_recv()
+
+    flat = jnp.sum(ky[...].astype(F32), axis=0).T
+    out_k[...] = jnp.concatenate([flat[g * TAPS : (g + 1) * TAPS, :] for g in range(3)], axis=1)
+
+    for half in range(2):
+        for col in range(2):
+            cols = slice(col * T, (col + 1) * T)
+            out_h[half, :, cols] = y_total(half, col, out_h[half, :, cols], (0,))
+
+    for way in range(2):
+        for side in range(2):
+            for col in range(2):
+                for half in range(2):
+                    r_copy(way, 1, half, side, col, y).wait_send()
 
     @pl.loop(1, 16)
     def _(off):
         k_copy(off, d).wait_send()
-
-    @pl.loop(1, 16)
-    def _(off):
-        k_copy(off, (d + off) % 16).wait_recv()
-
-    flat = jnp.sum(ky[...], axis=0).T
-    out_k[...] = jnp.concatenate([flat[g * TAPS : (g + 1) * TAPS, :] for g in range(3)], axis=1)
-
-    for half in range(2):
-        for col in range(2):
-            cx_copy(half, col).wait_recv()
-            cols = slice(col * T, (col + 1) * T)
-            out_h[half, :, cols] = out_h[half, :, cols] + xrin[half, col].astype(F32)
-
-    for half in range(2):
-        for col in range(2):
-            cx_copy(half, col).wait_send()
 
 
 def put_out(a, b, c, out_a, out_b, out_c, sem):
@@ -446,16 +455,14 @@
             pltpu.VMEM((VOC, T), BF),
             pltpu.VMEM((4, NZ, CH, T), BF),
             pltpu.VMEM((2, NZ, CH, T), BF),
-            pltpu.VMEM((NZ, CH, T), BF),
-            pltpu.VMEM((NZ, CH, T), BF),
-            pltpu.VMEM((NZ, CH, T), BF),
-            pltpu.VMEM((NZ, CH, T), BF),
+            pltpu.VMEM((2, NZ, CH, T), BF),
+            pltpu.VMEM((2, NZ, CH, T), BF),
             pltpu.VMEM((CH, T), F32),
+            pltpu.VMEM((2, 2, 2, CH, T), BF),
             pltpu.VMEM((2, 2, ZX, CH, T), BF),
             pltpu.VMEM((2, 4, 2, 2, 2, CH, T), BF),
             pltpu.VMEM((2, 2, CH, T), BF),
-            pltpu.VMEM((2, 2, CH, T), BF),
-            pltpu.VMEM((16, 16, 128), F32),
+            pltpu.VMEM((16, 16, 128), BF),
             dma((7,)),
             dma((31,)),
             dma((2, ZX)),
@@ -463,16 +470,15 @@
             dma((32,)),
             dma((2,)),
             dma((2,)),
-            dma((NZ,)),
-            dma((NZ,)),
-            dma((NZ,)),
-            dma((NZ,)),
+            dma((2, NZ)),
+            dma((2, NZ)),
             dma((2, 4, 2, 2, 2)),
             dma((2, 4, 2, 2, 2)),
             dma((2, 2)),
             dma((2, 2)),
             dma((16,)),
             dma((16,)),
+            pltpu.SemaphoreType.REGULAR,
         ],
         compiler_params=pltpu.CompilerParams(
             collective_id=0, has_side_effects=True, vmem_limit_bytes=24 * 1024 * 1024

time: 61.1 us -> 57.3 us (0.938)
  Pallas kernels: 59.7 us -> 55.9 us
    pallas_call x1, Pallas kernels: 59 us -> 55.1 us  [local(): pl.pallas_call(kernel, out_shape=shapes, in_specs=[pl.BlockSpec(memory_sp...]
where the time goes in v3:
time: 57.3 us; the launch traced here: 57.1 us
  Pallas kernels  55.9 us (98%)
  between operations  1.29 us (2%)
    pallas_call x1, Pallas kernels, local(): pl.pallas_call(kernel, out_shape=shapes, in_specs=[pl.BlockSpec(memory_sp...  55.1 us

profile of v3, /device:TPU:1, one launch (start us, length us, event | category | flops | bytes accessed | tf_op | source)
XLA Modules:
  0.0 57.1 jit_solution(18199360125563573210)
XLA Ops:
  1.3 55.1 %shard_map.103 = (f32[48,256]{1,0:T(8,128)S(1)}, f32[32,48]{1,0:T(8,128)S(1)}, f32[2,48,512]{2,1,0:T(8,128)S(1)}) custom-call(s32[1]{0:T(128)S(6)} %copy.11.used, bf16[48,256]{1,0:T(8,128)(2,1)} %bitcast.9, bf16[32,48]{1,0:T(8,128)(2,1)} %taps_hbm.1, bf16[8,2,2,48,512]{4,3,2,1,0:T(8,128)(2,1)} %bitcast.6, s32[1,256]{1,0:T(1,128)} %seg_hbm.1, ...), custom_call_target="tpu_custom_call" | custom-call | tf_op jit(solution)/shard_map/pallas_call | solution.py:431
  56.4 0.7 %shard_map.104 = (f32[48,256]{1,0:T(8,128)}, f32[32,48]{1,0:T(8,128)}, f32[2,48,512]{2,1,0:T(8,128)}) custom-call(f32[48,256]{1,0:T(8,128)S(1)} %get-tuple-element.9.a, f32[32,48]{1,0:T(8,128)S(1)} %get-tuple-element.10.b, f32[2,48,512]{2,1,0:T(8,128)S(1)} %get-tuple-element.11.c), custom_call_target="tpu_custom_call" | custom-call | tf_op jit(solution)/shard_map/pallas_call | solution.py:489

commit v4 on v3

--- a/solution.py
+++ b/solution.py
@@ -41,8 +41,8 @@
     w, wt, conv, xt, xm, src_rows, dst_rows, rel_ids, teach, tgt, ex, stats, gt,
     cg, cin, zsend, zin, grad,
     h4, hh, rin, xrin, ky,
-    in_sem, a_send, a_recv, b_send, b_recv, dc_send, dc_recv, dz_send, dz_recv,
-    r_send, r_recv, cx_send, cx_recv, k_send, k_recv, column_sem,
+    in_sem, a_send, a_recv, a_core, b_send, b_recv, dc_send, dc_recv, dz_send, dz_recv,
+    r_send, r_recv, r4_recv, r1_recv, cx_send, cx_recv, k_send, k_recv, column_sem,
 ):
     m = lax.axis_index("mp")
     d = lax.axis_index("dp")
@@ -119,22 +119,17 @@
         source = only(kept(delta), moved(xt[...], delta))
         xm[j] = source
         acc = acc + source * tap_t[:, j : j + 1]
-    conv[c, zx] = acc.astype(BF)
+    conv[c * ZX + zx] = acc.astype(BF)
 
     pl.semaphore_wait(barrier, len(near))
     pl.semaphore_signal(column_sem, inc=1, device_id=h_peer, device_id_type=MESH)
 
-    def a_copy(slot_c, slot_zx, k, peer):
-        return remote(
-            conv.at[slot_c, slot_zx], conv.at[slot_c, slot_zx], a_send.at[k], a_recv.at[slot_c, slot_zx], peer
-        )
-
-    sent = []
+    def a_copy(slot, peer):
+        block = conv.at[c * ZX + slot]
+        return remote(block, block, a_send, a_core if peer is core_peer else a_recv.at[slot], peer)
 
     def a_start(slot, peer):
-        copy = a_copy(c, slot, len(sent), peer)
-        copy.start()
-        sent.append(copy)
+        a_copy(slot, peer).start()
 
     a_start(zx, x_peer)
     a_start(zx, core_peer)
@@ -164,24 +159,27 @@
 
     def over(off):
         slot = z_at(off) * 2 + ox
-        a_copy(c, slot, 0, x_peer).wait_recv()
+        a_copy(slot, x_peer).wait_recv()
         a_start(slot, core_peer)
 
     over(0)
     for off in NEAR:
         slot = z_at(off) * 2 + xl
-        a_copy(c, slot, 0, z_peer(off)).wait_recv()
+        a_copy(slot, z_peer(off)).wait_recv()
         a_start(slot, x_peer)
         a_start(slot, core_peer)
     for off in NEAR:
         over(off)
-    logits = jnp.dot(wt[c], conv[c].reshape(ZX * CH, T), preferred_element_type=F32)
-
-    @pl.loop(0, ZX)
-    def _(slot):
-        a_copy(oc, slot, 0, core_peer).wait_recv()
-
-    logits = logits + jnp.dot(wt[oc], conv[oc].reshape(ZX * CH, T), preferred_element_type=F32)
+    def half_of(core):
+        return conv[pl.ds(core * ZX, ZX)].reshape(ZX * CH, T)
+
+    def several(ref, count, send, recv):
+        some = ref.at[pl.ds(0, count)]
+        return remote(some, some, send, recv, core_peer)
+
+    logits = jnp.dot(wt[c], half_of(c), preferred_element_type=F32)
+    several(conv, ZX, a_send, a_core).wait_recv()
+    logits = logits + jnp.dot(wt[oc], half_of(oc), preferred_element_type=F32)
 
     peak = jnp.max(logits, axis=0, keepdims=True)
     raised = jnp.exp(logits - peak)
@@ -191,19 +189,15 @@
 
     def b_copy(off, slot):
         return remote(
-            stats.at[slot], stats.at[slot], b_send.at[off], b_recv.at[slot], {"mp": (m + off) % 32}
+            stats.at[slot], stats.at[slot], b_send, b_recv, {"mp": (m + off) % 32}
         )
 
     @pl.loop(1, 32)
     def _(off):
         b_copy(off, m).start()
 
-    for copy in sent:
-        copy.wait_send()
-
-    @pl.loop(1, 32)
-    def _(off):
-        b_copy(off, (m + off) % 32).wait_recv()
+    several(conv, 31, a_send, a_core).wait_send()
+    several(stats, 31, b_send, b_recv).wait_recv()
 
     every = stats[...]
     most = jnp.max(every, axis=0)
@@ -215,13 +209,18 @@
     def row_of(side, owner):
         return (oh if side == 0 else xh) * NY + owner
 
+    def hh_at(half, col, side, owner):
+        return (half * 2 + col) * ZX + row_of(side, owner)
+
     def r_copy(way, dist, half, side, col, owner):
-        at = (way, dist - 1, half, side, col)
+        recv = r4_recv.at[way, side, col] if dist == 4 else r_recv.at[way, dist - 2, half, side, col]
+        if dist == 1:
+            recv = r1_recv.at[side]
         peer = y_peer(1 if way else -1)
         if dist == 1 and side == 0:
             peer = {"dp": oh * NY + y_at(1 if way else -1)}
-        src = h4.at[half, side, col] if dist == 4 else hh.at[half, col, row_of(side, owner)]
-        return remote(src, rin.at[at], r_send.at[at], r_recv.at[at], peer)
+        src = h4.at[half, side, col] if dist == 4 else hh.at[hh_at(half, col, side, owner)]
+        return remote(src, rin.at[way, dist - 1, half, side, col], r_send, recv, peer)
 
     def r_step(dist, late):
         for side in range(2):
@@ -233,15 +232,15 @@
                         continue
                     half = way if late else 1 - way
                     if dist < 3 or late:
-                        row = row_of(side, owner)
+                        row = hh_at(half, col, side, owner)
                         r_copy(way, dist + 1, half, side, col, owner).wait_recv()
-                        hh[half, col, row] = (
-                            hh[half, col, row].astype(F32) + rin[way, dist, half, side, col].astype(F32)
+                        hh[row] = (
+                            hh[row].astype(F32) + rin[way, dist, half, side, col].astype(F32)
                         ).astype(BF)
                     r_copy(way, dist, half, side, col, owner).start()
 
     spots = [(half, side) for half in range(2) for side in range(2)]
-    rows = jnp.concatenate([conv[half, row_of(side, y_at(4))] for half, side in spots])
+    rows = jnp.concatenate([conv[half * ZX + row_of(side, y_at(4))] for half, side in spots])
     for col in range(2):
         part = lax.dot_general(
             rows, gt[col * T : (col + 1) * T, :], (((1,), (1,)), ((), ())), preferred_element_type=F32
@@ -258,13 +257,13 @@
             k = side if core is oc else side + 2
             cg[k] = terms[side * NZ * CH : (side + 1) * NZ * CH].reshape(NZ, CH, T)
             if k < 2:
-                copy = remote(cg.at[k], cin.at[k], dc_send.at[k], dc_recv.at[k], core_peer)
+                copy = remote(cg.at[k], cin.at[k], dc_send, dc_recv.at[k], core_peer)
                 copy.start()
                 core_copies.append(copy)
 
     def d_copy(i, off):
         peer = {"mp": z_at(off) * 4 + (xl if i else ox) * 2 + c}
-        return remote(zsend.at[i, off], zin.at[i, off], dz_send.at[i, off], dz_recv.at[i, off], peer)
+        return remote(zsend.at[i * NZ + off], zin.at[i * NZ + off], dz_send, dz_recv, peer)
 
     d_moves = [(i, off) for i in range(2) for off in (*FAR, 0) if (i, off) != (1, 0)]
     core_copies[0].wait_recv()
@@ -272,15 +271,15 @@
         if (i, off) == (1, FAR[0]):
             core_copies[1].wait_recv()
         at = z_at(off)
-        zsend[i, off] = (cg[2 + i, at].astype(F32) + cin[i, at].astype(F32)).astype(BF)
+        zsend[i * NZ + off] = (cg[2 + i, at].astype(F32) + cin[i, at].astype(F32)).astype(BF)
         d_copy(i, off).start()
     grad[...] = cg[3, z].astype(F32) + cin[1, z].astype(F32)
 
     for half in range(2):
         for col in range(2):
-            hh[half, col] = (
+            hh[(half * 2 + col) * ZX : (half * 2 + col + 1) * ZX] = (
                 lax.dot_general(
-                    conv[half].reshape(ZX * CH, T),
+                    half_of(half),
                     gt[col * T : (col + 1) * T, :],
                     (((1,), (1,)), ((), ())),
                     preferred_element_type=F32,
@@ -290,27 +289,18 @@
             )
 
     r_step(3, False)
-    for side in range(2):
-        for col in range(2):
-            for way in range(2):
-                r_copy(way, 4, way, side, col, y).wait_send()
-
-    @pl.loop(1, 32)
-    def _(off):
-        b_copy(off, m).wait_send()
-
-    for copy in core_copies:
-        copy.wait_send()
+    several(stats, 31, b_send, b_recv).wait_send()
+    several(cg, 2, dc_send, dc_recv.at[0]).wait_send()
     r_step(3, True)
     r_step(2, False)
     r_step(2, True)
 
     def cx_copy(half, col):
         return remote(
-            hh.at[half, col, row_of(0, y)],
+            hh.at[hh_at(half, col, 0, y)],
             xrin.at[half, col],
-            cx_send.at[half, col],
-            cx_recv.at[half, col],
+            cx_send,
+            cx_recv,
             h_peer,
         )
 
@@ -320,9 +310,9 @@
     pl.semaphore_wait(column_sem, 1)
     r_step(1, False)
     conv_grad = grad[...]
+    several(zin, 15, dz_send, dz_recv).wait_recv()
     for i, off in d_moves:
-        d_copy(i, off).wait_recv()
-        conv_grad = conv_grad + zin[i, off].astype(F32)
+        conv_grad = conv_grad + zin[i * NZ + off].astype(F32)
     grad[...] = conv_grad
 
     group = lax.broadcasted_iota(jnp.int32, (1, 8, 128), 2)
@@ -335,7 +325,7 @@
     ky[d] = packed.reshape(16, 128).astype(BF)
 
     def k_copy(off, slot):
-        return remote(ky.at[slot], ky.at[slot], k_send.at[off], k_recv.at[slot], {"dp": (d + off) % 16})
+        return remote(ky.at[slot], ky.at[slot], k_send, k_recv, {"dp": (d + off) % 16})
 
     @pl.loop(1, 16)
     def _(off):
@@ -349,55 +339,34 @@
         acc = acc + only(kept(-delta), moved(grad[...], -delta) * tap_t[:, j : j + 1])
     out_in[...] = acc
 
-    for i, off in d_moves:
-        d_copy(i, off).wait_send()
-    for way in range(2):
-        for side in range(2):
-            for col in range(2):
-                for dist in range(2, 4):
-                    for half in range(2):
-                        r_copy(way, dist, half, side, col, y).wait_send()
+    several(zin, 15, dz_send, dz_recv).wait_send()
+    several(hh, 4, cx_send, cx_recv).wait_send()
+
+    several(hh, 4, cx_send, cx_recv).wait_recv()
+
+    def y_total(half, col, total, side):
+        for way in range(2):
+            total = total + rin[way, 0, half, side, col].astype(F32)
+        return total
+
+    several(hh, 8, r_send, r1_recv.at[1]).wait_recv()
     for half in range(2):
         for col in range(2):
-            cx_copy(half, col).wait_send()
-
-    def y_total(half, col, total, sides):
-        for side in sides:
-            for way in range(2):
-                r_copy(way, 1, half, side, col, y).wait_recv()
-                total = total + rin[way, 0, half, side, col].astype(F32)
-        return total
-
-    for half in range(2):
-        for col in range(2):
-            cx_copy(half, col).wait_recv()
-
-    for half in range(2):
-        for col in range(2):
-            total = hh[half, col, row_of(1, y)].astype(F32) + xrin[half, col].astype(F32)
-            out_h[half, :, col * T : (col + 1) * T] = y_total(half, col, total, (1,))
-
-    @pl.loop(1, 16)
-    def _(off):
-        k_copy(off, (d + off) % 16).wait_recv()
-
+            total = hh[hh_at(half, col, 1, y)].astype(F32) + xrin[half, col].astype(F32)
+            out_h[half, :, col * T : (col + 1) * T] = y_total(half, col, total, 1)
+
+    several(ky, 15, k_send, k_recv).wait_recv()
     flat = jnp.sum(ky[...].astype(F32), axis=0).T
     out_k[...] = jnp.concatenate([flat[g * TAPS : (g + 1) * TAPS, :] for g in range(3)], axis=1)
 
+    several(hh, 8, r_send, r1_recv.at[0]).wait_recv()
     for half in range(2):
         for col in range(2):
             cols = slice(col * T, (col + 1) * T)
-            out_h[half, :, cols] = y_total(half, col, out_h[half, :, cols], (0,))
-
-    for way in range(2):
-        for side in range(2):
-            for col in range(2):
-                for half in range(2):
-                    r_copy(way, 1, half, side, col, y).wait_send()
-
-    @pl.loop(1, 16)
-    def _(off):
-        k_copy(off, d).wait_send()
+            out_h[half, :, cols] = y_total(half, col, out_h[half, :, cols], 0)
+
+    several(hh, 56, r_send, r1_recv.at[0]).wait_send()
+    several(ky, 15, k_send, k_recv).wait_send()
 
 
 def put_out(a, b, c, out_a, out_b, out_c, sem):
@@ -442,7 +411,7 @@
             pltpu.VMEM((T,), F32),
             pltpu.VMEM((NZ, 2, 2, CH, VOC), BF),
             pltpu.VMEM((2, VOC, ZX * CH), BF),
-            pltpu.VMEM((2, ZX, CH, T), BF),
+            pltpu.VMEM((2 * ZX, CH, T), BF),
             pltpu.VMEM((CH, T), F32),
             pltpu.VMEM((TAPS, CH, T), F32),
             pltpu.VMEM((8, T), jnp.int32),
@@ -455,29 +424,32 @@
             pltpu.VMEM((VOC, T), BF),
             pltpu.VMEM((4, NZ, CH, T), BF),
             pltpu.VMEM((2, NZ, CH, T), BF),
-            pltpu.VMEM((2, NZ, CH, T), BF),
-            pltpu.VMEM((2, NZ, CH, T), BF),
+            pltpu.VMEM((2 * NZ, CH, T), BF),
+            pltpu.VMEM((2 * NZ, CH, T), BF),
             pltpu.VMEM((CH, T), F32),
             pltpu.VMEM((2, 2, 2, CH, T), BF),
-            pltpu.VMEM((2, 2, ZX, CH, T), BF),
+            pltpu.VMEM((4 * ZX, CH, T), BF),
             pltpu.VMEM((2, 4, 2, 2, 2, CH, T), BF),
             pltpu.VMEM((2, 2, CH, T), BF),
             pltpu.VMEM((16, 16, 128), BF),
             dma((7,)),
-            dma((31,)),
-            dma((2, ZX)),
-            dma((32,)),
-            dma((32,)),
+            dma,
+            dma((ZX,)),
+            dma,
+            dma,
+            dma,
+            dma,
             dma((2,)),
+            dma,
+            dma,
+            dma,
+            dma((2, 2, 2, 2, 2)),
+            dma((2, 2, 2)),
             dma((2,)),
-            dma((2, NZ)),
-            dma((2, NZ)),
-            dma((2, 4, 2, 2, 2)),
-            dma((2, 4, 2, 2, 2)),
-            dma((2, 2)),
-            dma((2, 2)),
-            dma((16,)),
-            dma((16,)),
+            dma,
+            dma,
+            dma,
+            dma,
             pltpu.SemaphoreType.REGULAR,
         ],
         compiler_params=pltpu.CompilerParams(

time: 57.3 us -> 54.7 us (0.955)
  Pallas kernels: 55.9 us -> 53.3 us
    pallas_call x1, Pallas kernels: 55.1 us -> 52.6 us  [local(): pl.pallas_call(kernel, out_shape=shapes, in_specs=[pl.BlockSpec(memory_sp...]
where the time goes in v4:
time: 54.7 us; the launch traced here: 54.6 us
  Pallas kernels  53.3 us (97%)
  between operations  1.29 us (2%)
    pallas_call x1, Pallas kernels, local(): pl.pallas_call(kernel, out_shape=shapes, in_specs=[pl.BlockSpec(memory_sp...  52.6 us

profile of v4, /device:TPU:1, one launch (start us, length us, event | category | flops | bytes accessed | tf_op | source)
XLA Modules:
  0.0 54.6 jit_solution(4670992180194531563)
XLA Ops:
  1.3 52.6 %shard_map.103 = (f32[48,256]{1,0:T(8,128)S(1)}, f32[32,48]{1,0:T(8,128)S(1)}, f32[2,48,512]{2,1,0:T(8,128)S(1)}) custom-call(s32[1]{0:T(128)S(6)} %copy.11.used, bf16[48,256]{1,0:T(8,128)(2,1)} %bitcast.9, bf16[32,48]{1,0:T(8,128)(2,1)} %taps_hbm.1, bf16[8,2,2,48,512]{4,3,2,1,0:T(8,128)(2,1)} %bitcast.6, s32[1,256]{1,0:T(1,128)} %seg_hbm.1, ...), custom_call_target="tpu_custom_call" | custom-call | tf_op jit(solution)/shard_map/pallas_call | solution.py:400
  53.9 0.7 %shard_map.104 = (f32[48,256]{1,0:T(8,128)}, f32[32,48]{1,0:T(8,128)}, f32[2,48,512]{2,1,0:T(8,128)}) custom-call(f32[48,256]{1,0:T(8,128)S(1)} %get-tuple-element.9.a, f32[32,48]{1,0:T(8,128)S(1)} %get-tuple-element.10.b, f32[2,48,512]{2,1,0:T(8,128)S(1)} %get-tuple-element.11.c), custom_call_target="tpu_custom_call" | custom-call | tf_op jit(solution)/shard_map/pallas_call | solution.py:461

commit v5 on v4

--- a/solution.py
+++ b/solution.py
@@ -39,9 +39,9 @@
     out_in, out_k, out_h,
     frames, taps, seg, ids, tlog, scale,
     w, wt, conv, xt, xm, src_rows, dst_rows, rel_ids, teach, tgt, ex, stats, gt,
-    cg, cin, zsend, zin, grad,
-    h4, hh, rin, xrin, ky,
-    in_sem, a_send, a_recv, a_core, b_send, b_recv, dc_send, dc_recv, dz_send, dz_recv,
+    cg, cin, xsend, xin, zsend, zin, grad,
+    first, hh, rin, xrin, ky,
+    in_sem, a_send, a_recv, a_core, b_send, b_recv, dc_send, dc_recv, dx_send, dx_recv, dz_send, dz_recv,
     r_send, r_recv, r4_recv, r1_recv, cx_send, cx_recv, k_send, k_recv, column_sem,
 ):
     m = lax.axis_index("mp")
@@ -219,7 +219,11 @@
         peer = y_peer(1 if way else -1)
         if dist == 1 and side == 0:
             peer = {"dp": oh * NY + y_at(1 if way else -1)}
-        src = h4.at[half, side, col] if dist == 4 else hh.at[hh_at(half, col, side, owner)]
+        src = hh.at[hh_at(half, col, side, owner)]
+        if dist == 4:
+            src = first.at[0, half, side, col]
+        if dist == 3 and half != way:
+            src = first.at[1, way, side, col]
         return remote(src, rin.at[way, dist - 1, half, side, col], r_send, recv, peer)
 
     def r_step(dist, late):
@@ -239,41 +243,57 @@
                         ).astype(BF)
                     r_copy(way, dist, half, side, col, owner).start()
 
-    spots = [(half, side) for half in range(2) for side in range(2)]
-    rows = jnp.concatenate([conv[half * ZX + row_of(side, y_at(4))] for half, side in spots])
+    core_copies = []
+
+    def terms_of(core, to):
+        rows = jnp.concatenate([w[:, side, core].reshape(NZ * CH, VOC) for side in (ox, xl)])
+        terms = jnp.dot(rows, gt[...], preferred_element_type=F32).astype(BF)
+        for side in range(2):
+            cg[to + side] = terms[side * NZ * CH : (side + 1) * NZ * CH].reshape(NZ, CH, T)
+
+    terms_of(oc, 0)
+    for k in range(2):
+        copy = remote(cg.at[k], cin.at[k], dc_send, dc_recv.at[k], core_peer)
+        copy.start()
+        core_copies.append(copy)
+
+    spots = [(half, side, 4) for half in range(2) for side in range(2)]
+    spots += [(1 - way, side, 3 if way else -3) for way in range(2) for side in range(2)]
+    rows = jnp.concatenate([conv[half * ZX + row_of(side, y_at(off))] for half, side, off in spots])
     for col in range(2):
         part = lax.dot_general(
             rows, gt[col * T : (col + 1) * T, :], (((1,), (1,)), ((), ())), preferred_element_type=F32
         ).astype(BF)
-        for k, (half, side) in enumerate(spots):
-            h4[half, side, col] = part[k * CH : (k + 1) * CH]
+        for k in range(len(spots)):
+            first[k // 4, k // 2 % 2, k % 2, col] = part[k * CH : (k + 1) * CH]
     r_step(4, True)
 
-    core_copies = []
-    for core in (oc, c):
-        rows = jnp.concatenate([w[:, side, core].reshape(NZ * CH, VOC) for side in (ox, xl)])
-        terms = jnp.dot(rows, gt[...], preferred_element_type=F32).astype(BF)
-        for side in range(2):
-            k = side if core is oc else side + 2
-            cg[k] = terms[side * NZ * CH : (side + 1) * NZ * CH].reshape(NZ, CH, T)
-            if k < 2:
-                copy = remote(cg.at[k], cin.at[k], dc_send, dc_recv.at[k], core_peer)
-                copy.start()
-                core_copies.append(copy)
+    terms_of(c, 2)
 
     def d_copy(i, off):
         peer = {"mp": z_at(off) * 4 + (xl if i else ox) * 2 + c}
         return remote(zsend.at[i * NZ + off], zin.at[i * NZ + off], dz_send, dz_recv, peer)
 
-    d_moves = [(i, off) for i in range(2) for off in (*FAR, 0) if (i, off) != (1, 0)]
+    d_near = [(i, off) for i in range(2) for off in (2, 6, 1, 7, 0) if (i, off) != (1, 0)]
+    d_far = (4, 3, 5)
+
+    def own_sum(i, at):
+        return cg[2 + i, at].astype(F32) + cin[i, at].astype(F32)
+
+    def dx_copy(k):
+        return remote(xsend.at[k], xin.at[k], dx_send, dx_recv, x_peer)
+
     core_copies[0].wait_recv()
-    for i, off in d_moves:
-        if (i, off) == (1, FAR[0]):
+    for k, off in enumerate(d_far):
+        xsend[k] = own_sum(0, z_at(off)).astype(BF)
+        dx_copy(k).start()
+    for i, off in d_near:
+        if (i, off) == (1, 2):
             core_copies[1].wait_recv()
-        at = z_at(off)
-        zsend[i * NZ + off] = (cg[2 + i, at].astype(F32) + cin[i, at].astype(F32)).astype(BF)
+        zsend[i * NZ + off] = own_sum(i, z_at(off)).astype(BF)
         d_copy(i, off).start()
-    grad[...] = cg[3, z].astype(F32) + cin[1, z].astype(F32)
+    grad[...] = own_sum(1, z)
+    r_step(3, False)
 
     for half in range(2):
         for col in range(2):
@@ -288,11 +308,15 @@
                 .reshape(ZX, CH, T)
             )
 
-    r_step(3, False)
     several(stats, 31, b_send, b_recv).wait_send()
     several(cg, 2, dc_send, dc_recv.at[0]).wait_send()
     r_step(3, True)
     r_step(2, False)
+    several(xin, 3, dx_send, dx_recv).wait_recv()
+    for k, off in enumerate(d_far):
+        zsend[NZ + off] = (own_sum(1, z_at(off)) + xin[k].astype(F32)).astype(BF)
+        d_copy(1, off).start()
+    several(xin, 3, dx_send, dx_recv).wait_send()
     r_step(2, True)
 
     def cx_copy(half, col):
@@ -310,8 +334,8 @@
     pl.semaphore_wait(column_sem, 1)
     r_step(1, False)
     conv_grad = grad[...]
-    several(zin, 15, dz_send, dz_recv).wait_recv()
-    for i, off in d_moves:
+    several(zin, 12, dz_send, dz_recv).wait_recv()
+    for i, off in d_near + [(1, off) for off in d_far]:
         conv_grad = conv_grad + zin[i * NZ + off].astype(F32)
     grad[...] = conv_grad
 
@@ -339,7 +363,7 @@
         acc = acc + only(kept(-delta), moved(grad[...], -delta) * tap_t[:, j : j + 1])
     out_in[...] = acc
 
-    several(zin, 15, dz_send, dz_recv).wait_send()
+    several(zin, 12, dz_send, dz_recv).wait_send()
     several(hh, 4, cx_send, cx_recv).wait_send()
 
     several(hh, 4, cx_send, cx_recv).wait_recv()
@@ -424,10 +448,12 @@
             pltpu.VMEM((VOC, T), BF),
             pltpu.VMEM((4, NZ, CH, T), BF),
             pltpu.VMEM((2, NZ, CH, T), BF),
+            pltpu.VMEM((3, CH, T), BF),
+            pltpu.VMEM((3, CH, T), BF),
             pltpu.VMEM((2 * NZ, CH, T), BF),
             pltpu.VMEM((2 * NZ, CH, T), BF),
             pltpu.VMEM((CH, T), F32),
-            pltpu.VMEM((2, 2, 2, CH, T), BF),
+            pltpu.VMEM((2, 2, 2, 2, CH, T), BF),
             pltpu.VMEM((4 * ZX, CH, T), BF),
             pltpu.VMEM((2, 4, 2, 2, 2, CH, T), BF),
             pltpu.VMEM((2, 2, CH, T), BF),
@@ -440,6 +466,8 @@
             dma,
             dma,
             dma((2,)),
+            dma,
+            dma,
             dma,
             dma,
             dma,

time: 54.7 us -> 54.4 us (level)
  no operation moved by 1% of the time
where the time goes in v5:
time: 54.4 us; the launch traced here: 54.2 us
  Pallas kernels  52.9 us (97%)
  between operations  1.29 us (2%)
    pallas_call x1, Pallas kernels, local(): pl.pallas_call(kernel, out_shape=shapes, in_specs=[pl.BlockSpec(memory_sp...  52.2 us

profile of v5, /device:TPU:1, one launch (start us, length us, event | category | flops | bytes accessed | tf_op | source)
XLA Modules:
  0.0 54.2 jit_solution(15229258279529402045)
XLA Ops:
  1.3 52.2 %shard_map.103 = (f32[48,256]{1,0:T(8,128)S(1)}, f32[32,48]{1,0:T(8,128)S(1)}, f32[2,48,512]{2,1,0:T(8,128)S(1)}) custom-call(s32[1]{0:T(128)S(6)} %copy.11.used, bf16[48,256]{1,0:T(8,128)(2,1)} %bitcast.9, bf16[32,48]{1,0:T(8,128)(2,1)} %taps_hbm.1, bf16[8,2,2,48,512]{4,3,2,1,0:T(8,128)(2,1)} %bitcast.6, s32[1,256]{1,0:T(1,128)} %seg_hbm.1, ...), custom_call_target="tpu_custom_call" | custom-call | tf_op jit(solution)/shard_map/pallas_call | solution.py:424
  53.5 0.7 %shard_map.104 = (f32[48,256]{1,0:T(8,128)}, f32[32,48]{1,0:T(8,128)}, f32[2,48,512]{2,1,0:T(8,128)}) custom-call(f32[48,256]{1,0:T(8,128)S(1)} %get-tuple-element.9.a, f32[32,48]{1,0:T(8,128)S(1)} %get-tuple-element.10.b, f32[2,48,512]{2,1,0:T(8,128)S(1)} %get-tuple-element.11.c), custom_call_target="tpu_custom_call" | custom-call | tf_op jit(solution)/shard_map/pallas_call | solution.py:489

commit v6 on v5

--- a/solution.py
+++ b/solution.py
@@ -187,14 +187,11 @@
     own = peak + jnp.log(jnp.sum(raised, axis=0, keepdims=True))
     stats[m] = own
 
-    def b_copy(off, slot):
-        return remote(
-            stats.at[slot], stats.at[slot], b_send, b_recv, {"mp": (m + off) % 32}
-        )
-
-    @pl.loop(1, 32)
-    def _(off):
-        b_copy(off, m).start()
+    for off in (*FAR, 0):
+        for side, core in ((ox, oc), (ox, c), (xl, oc), (xl, c)):
+            if off or side is not xl or core is not c:
+                peer = {"mp": z_at(off) * 4 + side * 2 + core}
+                remote(stats.at[m], stats.at[m], b_send, b_recv, peer).start()
 
     several(conv, 31, a_send, a_core).wait_send()
     several(stats, 31, b_send, b_recv).wait_recv()
@@ -348,12 +345,10 @@
             packed = jnp.where(group == g * TAPS + j, sums[2 * g : 2 * g + 2], packed)
     ky[d] = packed.reshape(16, 128).astype(BF)
 
-    def k_copy(off, slot):
-        return remote(ky.at[slot], ky.at[slot], k_send, k_recv, {"dp": (d + off) % 16})
-
-    @pl.loop(1, 16)
-    def _(off):
-        k_copy(off, d).start()
+    for off in (*FAR, 0):
+        for side in (oh, xh):
+            if off or side is not xh:
+                remote(ky.at[d], ky.at[d], k_send, k_recv, {"dp": side * NY + y_at(off)}).start()
 
     r_step(1, True)
 

time: 54.4 us -> 53.7 us (0.987)
  Pallas kernels: 52.9 us -> 52.3 us
    pallas_call x1, Pallas kernels: 52.2 us -> 51.6 us  [local(): pl.pallas_call(kernel, out_shape=shapes, in_specs=[pl.BlockSpec(memory_sp...]
where the time goes in v6:
time: 53.7 us; the launch traced here: 53.6 us
  Pallas kernels  52.3 us (97%)
  between operations  1.29 us (2%)
    pallas_call x1, Pallas kernels, local(): pl.pallas_call(kernel, out_shape=shapes, in_specs=[pl.BlockSpec(memory_sp...  51.6 us

profile of v6, /device:TPU:1, one launch (start us, length us, event | category | flops | bytes accessed | tf_op | source)
XLA Modules:
  0.0 53.6 jit_solution(897707708245863990)
XLA Ops:
  1.3 51.6 %shard_map.103 = (f32[48,256]{1,0:T(8,128)S(1)}, f32[32,48]{1,0:T(8,128)S(1)}, f32[2,48,512]{2,1,0:T(8,128)S(1)}) custom-call(s32[1]{0:T(128)S(6)} %copy.11.used, bf16[48,256]{1,0:T(8,128)(2,1)} %bitcast.9, bf16[32,48]{1,0:T(8,128)(2,1)} %taps_hbm.1, bf16[8,2,2,48,512]{4,3,2,1,0:T(8,128)(2,1)} %bitcast.6, s32[1,256]{1,0:T(1,128)} %seg_hbm.1, ...), custom_call_target="tpu_custom_call" | custom-call | tf_op jit(solution)/shard_map/pallas_call | solution.py:419
  52.9 0.7 %shard_map.104 = (f32[48,256]{1,0:T(8,128)}, f32[32,48]{1,0:T(8,128)}, f32[2,48,512]{2,1,0:T(8,128)}) custom-call(f32[48,256]{1,0:T(8,128)S(1)} %get-tuple-element.9.a, f32[32,48]{1,0:T(8,128)S(1)} %get-tuple-element.10.b, f32[2,48,512]{2,1,0:T(8,128)S(1)} %get-tuple-element.11.c), custom_call_target="tpu_custom_call" | custom-call | tf_op jit(solution)/shard_map/pallas_call | solution.py:484
